TPU v7x, 128 devices: a whole 4x4x4 slice. The times are simulated.
128 devices in a mesh: blk: 16 (over y, z), rep: 8 (over x, core).
Axes of the slice: x: 4, y: 4, z: 4, core: 2. Of those that a mesh axis runs over, the one named last changes fastest.
Arguments:
- dense: bfloat16 [131072, 1024], P(('blk', 'rep')), may hold values from -6 to 6
- labels: int32 [131072], P(('blk', 'rep')), may hold values 0 or 1
- tile_values: bfloat16 [16384, 64, 128], P(('blk', 'rep')), may hold values from -1.1953125 to 1.1953125
- tile_block: int32 [16384, 64], P(('blk', 'rep')), may hold values from 0 to 1023
- tile_example: int32 [16384, 64], P(('blk', 'rep')), may hold values from 0 to 1023
- tile_count: int32 [16384], P(('blk', 'rep')), may hold values from 16 to 64, as said below
- z_state: float32 [131072, 128], P(('blk', 'rep')), may hold values from -6 to 6
- n_state: float32 [131072, 128], P(('blk', 'rep')), may hold values from 0.01 to 4
- w_one: bfloat16 [1024, 512], replicated, may hold values from -0.1875 to 0.1875
- b_one: float32 [512], replicated, may hold values from -3 to 3
- w_two: bfloat16 [512, 256], replicated, may hold values from -0.25 to 0.25
- b_two: float32 [256], replicated, may hold values from -3 to 3
- head: bfloat16 [256], replicated, may hold values from -0.375 to 0.375
Outputs:
- probability: float32 [131072], P(('blk', 'rep'))
- z_new: float32 [131072, 128], P(('blk', 'rep'))
- n_new: float32 [131072, 128], P(('blk', 'rep'))
- grad_w_one: float32 [1024, 512], replicated
- grad_b_one: float32 [512], replicated
- grad_w_two: float32 [512, 256], replicated
- grad_b_two: float32 [256], replicated
- grad_head: float32 [256], replicated
Inputs may be any that keep to these rules, and one draw needn't show every extreme that they name: `tile_count`: slots at or beyond a list's count are padding; in every draw some owners receive 64 live slots from every device.
All inputs are finite; a program needn't handle non-finite values. No bound on the sum of `labels` on one device may be relied on, other than what follows from the above.
Results may differ from a plain program's by a relative error of at most 0.013.
Values may be sent and summed in bfloat16 or wider, within the bound.
A program may use at most 64 MiB of HBM per device.

v0:
```python
import jax
import jax.numpy as jnp
from jax import lax
from jax.sharding import PartitionSpec as P

alpha_rate = 0.5
beta_shift = 1.0
lasso_term = 0.5
ridge_term = 0.1


def wide_weight(z_state, n_state):
    shrunk = z_state - jnp.sign(z_state) * lasso_term
    denominator = (beta_shift + jnp.sqrt(n_state)) / alpha_rate + ridge_term
    return jnp.where(jnp.abs(z_state) > lasso_term, -shrunk / denominator, jnp.zeros_like(z_state))


def silu_slope(pre):
    gate = jax.nn.sigmoid(pre)
    return gate * (1.0 + pre * (1.0 - gate))


def per_device(
    dense,
    labels,
    tile_values,
    tile_block,
    tile_example,
    tile_count,
    z_state,
    n_state,
    w_one,
    b_one,
    w_two,
    b_two,
    head,
):
    owners, capacity, width = tile_values.shape
    slots = jnp.arange(capacity, dtype=jnp.int32)
    live = slots[None, :] < tile_count[:, None]
    masked = jnp.where(live[:, :, None], tile_values, jnp.zeros_like(tile_values))
    got_values, got_block = (
        lax.all_to_all(masked, ("blk", "rep"), split_axis=0, concat_axis=0, tiled=True),
        lax.all_to_all(tile_block, ("blk", "rep"), split_axis=0, concat_axis=0, tiled=True),
    )
    weight = wide_weight(z_state, n_state)
    flat_block = got_block.reshape(-1)
    flat_values = got_values.reshape(-1, width)
    picked = jnp.take(weight, flat_block, axis=0)
    tile_logit = jnp.sum(flat_values.astype(jnp.float32) * picked, axis=1).reshape(owners, capacity)
    returned = lax.all_to_all(tile_logit, ("blk", "rep"), split_axis=0, concat_axis=0, tiled=True)
    flat_example = tile_example.reshape(-1)
    wide = jnp.zeros((dense.shape[0],), jnp.float32).at[flat_example].add(returned.reshape(-1))
    pre_one = jnp.dot(dense, w_one, preferred_element_type=jnp.float32) + b_one
    hid_one = jax.nn.silu(pre_one).astype(jnp.bfloat16)
    pre_two = jnp.dot(hid_one, w_two, preferred_element_type=jnp.float32) + b_two
    hid_two = jax.nn.silu(pre_two).astype(jnp.bfloat16)
    deep = jnp.dot(hid_two, head, preferred_element_type=jnp.float32)
    probability = jax.nn.sigmoid(wide + deep)
    residual = probability - labels.astype(jnp.float32)
    tile_residual = jnp.take(residual, flat_example).reshape(owners, capacity)
    got_residual = lax.all_to_all(
        tile_residual, ("blk", "rep"), split_axis=0, concat_axis=0, tiled=True
    )
    contrib = flat_values.astype(jnp.float32) * got_residual.reshape(-1)[:, None]
    grad_block = jnp.zeros_like(z_state).at[flat_block].add(contrib)
    n_new = n_state + grad_block * grad_block
    sigma = (jnp.sqrt(n_new) - jnp.sqrt(n_state)) / alpha_rate
    z_new = z_state + grad_block - sigma * weight
    dlogit = residual.astype(jnp.bfloat16)
    grad_head = jnp.dot(dlogit, hid_two, preferred_element_type=jnp.float32)
    d_two = (
        dlogit.astype(jnp.float32)[:, None]
        * head.astype(jnp.float32)[None, :]
        * silu_slope(pre_two)
    ).astype(jnp.bfloat16)
    grad_w_two = lax.dot_general(
        hid_one, d_two, (((0,), (0,)), ((), ())), preferred_element_type=jnp.float32
    )
    grad_b_two = jnp.sum(d_two.astype(jnp.float32), axis=0)
    back_one = lax.dot_general(
        d_two, w_two, (((1,), (1,)), ((), ())), preferred_element_type=jnp.float32
    )
    d_one = (back_one * silu_slope(pre_one)).astype(jnp.bfloat16)
    grad_w_one = lax.dot_general(
        dense, d_one, (((0,), (0,)), ((), ())), preferred_element_type=jnp.float32
    )
    grad_b_one = jnp.sum(d_one.astype(jnp.float32), axis=0)
    grad_head, grad_w_two, grad_b_two, grad_w_one, grad_b_one = lax.psum(
        (grad_head, grad_w_two, grad_b_two, grad_w_one, grad_b_one), ("blk", "rep")
    )
    return (probability, z_new, n_new, grad_w_one, grad_b_one, grad_w_two, grad_b_two, grad_head)


def solution(mesh):
    placed = (
        P(("blk", "rep"), None),
        P(("blk", "rep")),
        P(("blk", "rep"), None, None),
        P(("blk", "rep"), None),
        P(("blk", "rep"), None),
        P(("blk", "rep")),
        P(("blk", "rep"), None),
        P(("blk", "rep"), None),
        P(),
        P(),
        P(),
        P(),
        P(),
    )
    return jax.shard_map(
        per_device,
        mesh=mesh,
        in_specs=placed,
        out_specs=(
            P(("blk", "rep")),
            P(("blk", "rep"), None),
            P(("blk", "rep"), None),
            P(),
            P(),
            P(),
            P(),
            P(),
        ),
        check_vma=False,
    )
```

profile of v0, /device:TPU:1, one launch (start us, length us, event | category | flops | bytes accessed | tf_op | source)
XLA Modules:
  0.0 373.5 jit_solution(6273867925865264041)
XLA Ops:
  7.2 0.0 copy-start
  7.2 1.6 copy.30
  8.8 11.5 %all-to-all-start.1 = ((s32[128,1,64]{2,1,0:T(1,128)}), s32[128,1,64]{2,1,0:T(1,128)S(1)}, u32[]{:S(2)}, u32[]{:S(2)}) async-start(s32[128,1,64]{2,1,0:T(1,128)} %bitcast.2), calls=%async_computation.1 | async-start | bytes 131072 | tf_op jit(solution)/shard_map/all_to_all | solution.py:44
  20.3 0.7 iota_compare_fusion
  21.1 0.7 reshape.183
  21.7 0.8 copy.29
  22.6 0.1 reshape.146
  22.7 1.6 divide_select_fusion
  24.4 0.0 copy-start.5
  24.4 0.0 copy-start.8
  24.4 4.5 %broadcast_select_fusion = bf16[128,64,128]{2,1,0:T(8,128)(2,1)} fusion(bf16[128,64,128]{2,1,0:T(8,128)(2,1)} %param.15, pred[128,64]{1,0:T(8,128)(4,1)S(1)} %iota_compare_fusion), kind=kLoop, calls=%fused_computation.10 | loop fusion | flops 1048576 | bytes 4202496 | tf_op jit(solution)/shard_map/jit(_where)/select_n | solution.py:41
  28.9 0.0 copy-done
  28.9 0.0 copy-done.5
  28.9 0.0 copy-done.8
  28.9 0.0 copy-start.6
  28.9 0.0 copy-start.9
  29.0 2.8 multiply_convert_fusion.1
  31.7 0.0 copy-done.6
  31.7 0.0 copy-done.9
  31.7 1.4 multiply_convert_fusion.3
  33.1 0.0 copy-done.11
  33.1 0.2 fusion.3
  33.4 0.0 all-to-all-done.1
  33.4 10.2 %all-to-all-start = ((bf16[128,64,128]{2,1,0:T(8,128)(2,1)}), bf16[128,64,128]{2,1,0:T(8,128)(2,1)}, u32[]{:S(2)}, u32[]{:S(2)}) async-start(bf16[128,64,128]{2,1,0:T(8,128)(2,1)} %broadcast_select_fusion), calls=%async_computation | async-start | bytes 4194304 | tf_op jit(solution)/shard_map/all_to_all | solution.py:43
  43.6 0.5 broadcast.153
  44.1 0.8 reduce.10
  44.9 0.1 reshape.148
  45.1 27.8 %gather_fusion = f32[8192,128]{1,0:T(8,128)} fusion(f32[1024,128]{1,0:T(8,128)S(1)} %divide_select_fusion, s32[8192]{0:T(1024)S(1)} %broadcast_clamp_fusion.1), kind=kCustom, calls=%fused_computation | custom fusion | bytes 8421376 | tf_op jit(solution)/shard_map/jit(_take)/gather | solution.py:49
  72.9 0.9 all-to-all-done
  73.8 5.4 %multiply_reduce_fusion = f32[128,64]{1,0:T(8,128)} fusion(f32[128,64,128]{2,1,0:T(8,128)} %bitcast.30, pred[128,64]{1,0:T(8,128)(4,1)S(1)} %compare_and_fusion, bf16[128,64,128]{2,1,0:T(8,128)(2,1)} %all-to-all-done), kind=kLoop, calls=%fused_computation.5 | loop fusion | flops 4186112 | bytes 6332416 | tf_op jit(solution)/shard_map/reduce_sum | solution.py:50
  79.2 8.9 %all-to-all-start.2 = ((f32[128,1,64]{2,1,0:T(1,128)}), f32[128,1,64]{2,1,0:T(1,128)S(1)}, u32[]{:S(2)}, u32[]{:S(2)}) async-start(f32[128,1,64]{2,1,0:T(1,128)} %bitcast.6), calls=%async_computation.2 | async-start | bytes 131072 | tf_op jit(solution)/shard_map/all_to_all | solution.py:51
  88.1 0.0 copy-done.10
  88.2 9.4 %all-to-all-done.2 = f32[128,1,64]{2,1,0:T(1,128)S(1)} async-done(((f32[128,1,64]{2,1,0:T(1,128)}), f32[128,1,64]{2,1,0:T(1,128)S(1)}, u32[]{:S(2)}, u32[]{:S(2)}) %all-to-all-start.2) | async-done | bytes 32800 | tf_op jit(solution)/shard_map/all_to_all | solution.py:51
  97.5 0.5 broadcast.154
  98.0 0.8 reduce.11
  98.9 0.1 reshape.171
  98.9 57.0 %scatter_fusion = f32[1024]{0:T(1024)S(1)} fusion(f32[1024]{0:T(1024)S(1)} %bitcast.29, s32[8192]{0:T(1024)S(1)} %bitcast.33, f32[8192]{0:T(1024)S(1)} %reshape.171), kind=kCustom, calls=%fused_computation.2 | custom fusion | flops 8192 | bytes 131072 | tf_op jit(solution)/shard_map/scatter-add | solution.py:53
  155.9 0.0 copy-done.4
  156.0 0.0 copy-start.7
  156.0 0.0 copy-start.12
  156.0 0.6 fusion.2
  156.6 1.8 convert_reduce_fusion.1
  158.3 2.5 fusion.4
  160.8 0.0 copy-done.7
  160.8 0.0 copy-done.12
  160.8 1.0 convert_reduce_fusion
  161.9 2.6 convolution_bitcast_fusion
  164.5 32.9 %gather_fusion.1 = f32[8192]{0:T(1024)S(1)} fusion(f32[1024]{0:T(1024)S(1)} %get-tuple-element.41, s32[8192]{0:T(1024)S(1)} %broadcast_clamp_fusion), kind=kCustom, calls=%fused_computation.1 | custom fusion | bytes 98304 | tf_op jit(solution)/shard_map/jit(_take)/gather | solution.py:61
  197.4 0.1 gather.15
  197.4 0.7 and_select_fusion
  198.1 4.6 %all-to-all-start.3 = ((f32[128,1,64]{2,1,0:T(1,128)}), f32[128,1,64]{2,1,0:T(1,128)S(1)}, u32[]{:S(2)}, u32[]{:S(2)}) async-start(f32[128,1,64]{2,1,0:T(1,128)} %bitcast.9), calls=%async_computation.3 | async-start | bytes 131072 | tf_op jit(solution)/shard_map/all_to_all | solution.py:62
  202.7 0.0 all-reduce.4.cloned.1.call-start
  202.8 0.2 fusion.5
  202.9 0.5 all-reduce.4.cloned.1.call-update
  203.4 67.4 %all-reduce = (f32[512]{0:T(512)}, f32[256]{0:T(256)}, f32[256]{0:T(256)}) all-reduce(f32[512]{0:T(512)S(1)} %get-tuple-element.49, f32[256]{0:T(256)S(1)} %get-tuple-element.37, f32[256]{0:T(256)S(1)} %bitcast.36), channel_id=1, replica_groups=mesh['blk'=16,'rep'=8] {'blk','rep'}, use_global_device_ids=true, to_apply=%region_5.6 | all-reduce | flops 1024 | bytes 8192 | tf_op jit(solution)/shard_map/psum | solution.py:89
  270.9 0.0 all-to-all-done.3
  270.9 0.8 reduce.12
  271.7 0.1 mul.66
  271.8 3.9 %bitcast_multiply_fusion = f32[8192,128]{1,0:T(8,128)} fusion(f32[8192]{0:T(1024)S(1)} %mul.66, bf16[128,64,128]{2,1,0:T(8,128)(2,1)} %all-to-all-done), kind=kLoop, calls=%fused_computation.4 | loop fusion | flops 2097152 | bytes 6324224 | tf_op jit(solution)/shard_map/mul | solution.py:65
  275.7 45.1 %scatter_custom_fusion.1 = f32[1024,128]{1,0:T(8,128)} fusion(s32[8192]{0:T(1024)S(1)} %bitcast.35, f32[8192,128]{1,0:T(8,128)} %bitcast_multiply_fusion, f32[]{:T(128)} %constant.32.clone.1), kind=kCustom, calls=%fused_computation.21 | custom fusion | flops 1048576 | bytes 524800 | tf_op jit(solution)/shard_map/scatter-add | solution.py:66
  320.7 2.7 multiply_subtract_fusion
  323.4 39.5 %all-reduce.4.cloned.1.call-done = (f32[1024,512]{0,1:T(8,128)}, f32[512,256]{1,0:T(8,128)}) async-done(((f32[1024,512]{0,1:T(8,128)}, f32[512,256]{1,0:T(8,128)}), (f32[1024,512]{0,1:T(8,128)}, f32[512,256]{1,0:T(8,128)})) %all-reduce.4.cloned.1.call-update) | async-done | bytes 2621456 | tf_op jit(solution)/shard_map/psum | solution.py:89
  362.9 2.9 copy.35
  365.8 0.8 copy.39
  (16 shorter events, 0.1 us)
Async XLA Ops:
  7.2 21.8 %copy-start = (bf16[1024,1024]{1,0:T(8,128)(2,1)S(1)}, bf16[1024,1024]{1,0:T(8,128)(2,1)}, u32[]{:S(2)}) copy-start(bf16[1024,1024]{1,0:T(8,128)(2,1)} %param.13) | copy-start | bytes 6291460
  8.8 24.6 %all-to-all-start.1 = ((s32[128,1,64]{2,1,0:T(1,128)}), s32[128,1,64]{2,1,0:T(1,128)S(1)}, u32[]{:S(2)}, u32[]{:S(2)}) async-start(s32[128,1,64]{2,1,0:T(1,128)} %bitcast.2), calls=%async_computation.1 | async-start | bytes 131072 | tf_op jit(solution)/shard_map/all_to_all | solution.py:44
  24.4 4.6 %copy-start.5 = (bf16[1024,512]{1,0:T(8,128)(2,1)S(1)}, bf16[1024,512]{1,0:T(8,128)(2,1)}, u32[]{:S(2)}) copy-start(bf16[1024,512]{1,0:T(8,128)(2,1)} %param.21) | copy-start | bytes 3145732
  24.4 4.5 %copy-start.8 = (f32[512]{0:T(512)S(1)}, f32[512]{0:T(512)}, u32[]{:S(2)}) copy-start(f32[512]{0:T(512)} %param.22) | copy-start | bytes 6148
  28.9 2.8 copy-start.6
  28.9 2.8 copy-start.9
  31.7 1.4 copy-start.11
  33.4 40.4 %all-to-all-start = ((bf16[128,64,128]{2,1,0:T(8,128)(2,1)}), bf16[128,64,128]{2,1,0:T(8,128)(2,1)}, u32[]{:S(2)}, u32[]{:S(2)}) async-start(bf16[128,64,128]{2,1,0:T(8,128)(2,1)} %broadcast_select_fusion), calls=%async_computation | async-start | bytes 4194304 | tf_op jit(solution)/shard_map/all_to_all | solution.py:43
  73.8 14.3 %copy-start.10 = (bf16[256]{0:T(256)(128)(2,1)S(1)}, bf16[256]{0:T(256)(128)(2,1)}, u32[]{:S(2)}) copy-start(bf16[256]{0:T(256)(128)(2,1)} %param.25) | copy-start | bytes 1540
  79.2 18.3 %all-to-all-start.2 = ((f32[128,1,64]{2,1,0:T(1,128)}), f32[128,1,64]{2,1,0:T(1,128)S(1)}, u32[]{:S(2)}, u32[]{:S(2)}) async-start(f32[128,1,64]{2,1,0:T(1,128)} %bitcast.6), calls=%async_computation.2 | async-start | bytes 131072 | tf_op jit(solution)/shard_map/all_to_all | solution.py:51
  98.9 57.0 %copy-start.4 = (s32[1024]{0:T(1024)S(1)}, s32[1024]{0:T(1024)}, u32[]{:S(2)}) copy-start(s32[1024]{0:T(1024)} %param.14) | copy-start | bytes 12292
  156.0 4.9 %copy-start.7 = (bf16[512,256]{1,0:T(8,128)(2,1)S(1)}, bf16[512,256]{1,0:T(8,128)(2,1)}, u32[]{:S(2)}) copy-start(bf16[512,256]{1,0:T(8,128)(2,1)} %param.23) | copy-start | bytes 786436
  156.0 4.9 %copy-start.12 = (f32[1024,512]{1,0:T(8,128)S(1)}, f32[1024,512]{1,0:T(8,128)}, u32[]{:S(2)}) copy-start(f32[1024,512]{1,0:T(8,128)} %get-tuple-element.46) | copy-start | bytes 6291460
  198.1 72.8 %all-to-all-start.3 = ((f32[128,1,64]{2,1,0:T(1,128)}), f32[128,1,64]{2,1,0:T(1,128)S(1)}, u32[]{:S(2)}, u32[]{:S(2)}) async-start(f32[128,1,64]{2,1,0:T(1,128)} %bitcast.9), calls=%async_computation.3 | async-start | bytes 131072 | tf_op jit(solution)/shard_map/all_to_all | solution.py:62
  202.7 160.2 %all-reduce.4.cloned.1.call-start = ((), (), s32[]{:S(2)}) async-start(), calls=%async_computation.4 | async-start | bytes 5242880 | tf_op jit(solution)/shard_map/psum | solution.py:89
  271.8 49.0 %copy-start.1 = (f32[1024,128]{1,0:T(8,128)S(1)}, f32[1024,128]{1,0:T(8,128)}, u32[]{:S(2)}) copy-start(f32[1024,128]{1,0:T(8,128)} %param.19) | copy-start | bytes 1572868
  271.8 49.0 %copy-start.2 = (f32[1024,128]{1,0:T(8,128)S(1)}, f32[1024,128]{1,0:T(8,128)}, u32[]{:S(2)}) copy-start(f32[1024,128]{1,0:T(8,128)} %param.20) | copy-start | bytes 1572868
  362.9 2.9 copy-start.3
Sparse Core Ops, SparseCore 0:
  209.1 153.7 all-reduce.3
where the time goes:
time: 374 us; the launch traced here: 373 us
  other arithmetic  127 us (34%)
  local copies, waits for them, and re-layouts  69 us (18%)
  blocking collectives  67.4 us (18%)
  waiting for transfers between devices  50.3 us (13%)
  starting transfers between devices  35.3 us (9%)
  between operations  14.3 us (4%)
  matrix products  10.7 us (3%)
    psum x1, blocking collectives, per_device(): lax.psum((grad_head, grad_w_two, grad_b_two, grad_w_one, grad_b_one), ('b...  67.4 us
    scatter-add x1, other arithmetic, per_device(): jnp.zeros((dense.shape[0],), jnp.float32).at[flat_example]  57 us
    scatter-add x1, other arithmetic, per_device(): grad_block = jnp.zeros_like(z_state).at[flat_block].add(contrib)  45.1 us
    psum x1, waiting for transfers between devices, per_device(): lax.psum((grad_head, grad_w_two, grad_b_two, grad_w_one, grad_b_one), ('b...  39.5 us
    gather x2, local copies, waits for them, and re-layouts, per_device(): tile_residual = jnp.take(residual, flat_example).reshape(owners, capacity)  32.9 us
    gather x1, local copies, waits for them, and re-layouts, per_device(): picked = jnp.take(weight, flat_block, axis=0)  27.8 us
    all_to_all x1, starting transfers between devices, per_device(): lax.all_to_all(tile_block, ('blk', 'rep'), split_axis=0, concat_axis=0, t...  11.5 us
    all_to_all x1, starting transfers between devices, per_device(): lax.all_to_all(masked, ('blk', 'rep'), split_axis=0, concat_axis=0, tiled...  10.2 us
  transfers between devices with their start and end apart: 5, of which 3 were waited for; matrix products, arithmetic and copies ran while one was open for 25% of the time, Pallas kernels for 0%

commit v1 on v0

v1 whole, which is shorter than its diff:
```python
import functools

import jax
import jax.numpy as jnp
from jax import lax
from jax.experimental import pallas as pl
from jax.experimental.pallas import tpu as pltpu
from jax.sharding import PartitionSpec as P

MESH = pl.DeviceIdType.MESH
F32 = jnp.float32
BF16 = jnp.bfloat16
NT = (((1,), (1,)), ((), ()))


def mm(a, b):
    return jnp.dot(a, b, preferred_element_type=F32)


def mm_nt(a, b):
    return lax.dot_general(a, b, NT, preferred_element_type=F32)


def step_kernel(
    B, R,
    dense_h, labels_h, values_h, index_h, example_h, z_h, n_h,
    w_one_h, b_one_h, w_two_h, b_two_h, head_h,
    prob_o, z_o, n_o, g_one_o, g_two_o, small_o,
    dense_v, labels_v, example_v, z_v, n_v, w_one_v, b_one_v, w_two_v, b_two_v, head_v,
    got_values, got_index, weight_v, weight_pair,
    hid_two_v, dense_t, hid_one_t, scale_one, scale_two, deep_v, low_hot,
    logit_send, logit_got, spread, picked, res_send, res_got,
    block_hot, total, z_out_v, n_out_v,
    d_one_v, d_two_v,
    part_one, part_two, own_one, pair_one, pair_two,
    sum_one, sum_two, got_one, got_two, fin_one, fin_two, full_one, full_two,
    small_v, small_rep, small_sum, small_blk,
    load_sem, own_sem, index_sem, value_sem, logit_sem, res_sem,
    pair_sem, rs_sem, ag_sem, fw_sem, small_sem,
    send_sem, out_sem,
):
    ND = B * R
    NC = ND // 2
    X = R // 2
    E, DIN = dense_v.shape
    H1 = w_one_v.shape[1]
    H2 = w_two_v.shape[1]
    CAP, W = got_values.shape[1], got_values.shape[2]
    BD = z_v.shape[0]
    NH = E // 128
    NP = ND // 2
    c1 = DIN * H1 // (128 * ND)
    c2 = H1 * H2 // (128 * ND)
    j1 = H1 // 128
    j2 = H2 // 128
    blk = lax.axis_index("blk")
    rep = lax.axis_index("rep")
    core = rep % 2
    other = 1 - core
    me = blk * R + rep
    chip = blk * X + rep // 2

    loads = [
        (z_h, z_v), (n_h, n_v), (dense_h, dense_v), (w_one_h, w_one_v), (b_one_h, b_one_v),
        (w_two_h, w_two_v), (b_two_h, b_two_v), (head_h, head_v), (example_h, example_v), (labels_h, labels_v),
    ]
    copies = [pltpu.make_async_copy(s, d, load_sem.at[i]) for i, (s, d) in enumerate(loads)]
    for copy in copies:
        copy.start()
    own_value = pltpu.make_async_copy(values_h.at[me], got_values.at[me], own_sem.at[0])
    own_value.start()
    own_index = pltpu.make_async_copy(index_h.at[me], got_index.at[me], own_sem.at[1])
    own_index.start()

    def send(src, dst, sem_at, recv, where):
        pltpu.make_async_remote_copy(
            src_ref=src, dst_ref=dst, send_sem=send_sem.at[sem_at], recv_sem=recv,
            device_id=where, device_id_type=MESH,
        ).start()

    def wait_for(ref, sem):
        pltpu.make_async_copy(ref, ref, sem).wait()

    barrier = pltpu.get_barrier_semaphore()

    @pl.loop(1, ND)
    def _(k):
        there = lax.rem(me + k, ND)
        pl.semaphore_signal(barrier, inc=1, device_id=(there // R, lax.rem(there, R)), device_id_type=MESH)

    copies[0].wait()
    copies[1].wait()
    z = z_v[...]
    shrunk = z - jnp.where(z > 0, 0.5, -0.5)
    weight = jnp.where(jnp.abs(z) > 0.5, -shrunk / ((1.0 + jnp.sqrt(n_v[...])) / 0.5 + 0.1), 0.0)
    weight_v[...] = weight
    high = weight.astype(BF16)
    weight_pair[:, :W] = high
    weight_pair[:, W:] = (weight - high.astype(F32)).astype(BF16)

    pl.semaphore_wait(barrier, ND - 1)

    @pl.loop(1, ND)
    def _(k):
        blk_to = lax.rem(blk + k // R, B)
        rep_to = lax.rem(rep + lax.rem(k, R), R)
        to = blk_to * R + rep_to
        send(index_h.at[to], got_index.at[me], 0, index_sem, (blk_to, rep_to))

    @pl.loop(1, ND)
    def _(k):
        blk_to = lax.rem(blk + k // R, B)
        rep_to = lax.rem(rep + lax.rem(k, R), R)
        to = blk_to * R + rep_to
        send(values_h.at[to], got_values.at[me], 1, value_sem.at[k // R], (blk_to, rep_to))

    for copy in copies[2:]:
        copy.wait()
    rows = 256
    head_rows = jnp.broadcast_to(head_v[...], (8, H2))

    @pl.loop(0, E // rows)
    def _(i):
        at = pl.multiple_of(i * rows, rows)
        dense = dense_v[pl.ds(at, rows), :]
        pre_one = mm(dense, w_one_v[...]) + b_one_v[...]
        gate_one = jax.nn.sigmoid(pre_one)
        hid_one = (pre_one * gate_one).astype(BF16)
        pre_two = mm(hid_one, w_two_v[...]) + b_two_v[...]
        gate_two = jax.nn.sigmoid(pre_two)
        hid_two = (pre_two * gate_two).astype(BF16)
        hid_two_v[pl.ds(at, rows), :] = hid_two
        two = head_v[...].astype(F32) * (gate_two * (1.0 + pre_two * (1.0 - gate_two)))
        scale_two[pl.ds(at, rows), :] = two
        back = mm_nt(two.astype(BF16), w_two_v[...])
        scale_one[pl.ds(at, rows), :] = back * (gate_one * (1.0 + pre_one * (1.0 - gate_one)))
        deep = mm_nt(head_rows, hid_two)
        for q in range(rows // 128):
            deep_v[pl.ds(i * (rows // 128) + q, 1), :] = deep[0:1, q * 128:(q + 1) * 128]
        dense_t[:, pl.ds(at, rows)] = dense.T
        hid_one_t[:, pl.ds(at, rows)] = hid_one.T

    @pl.loop(0, NP)
    def _(p):
        at = pl.multiple_of(p * 128, 128)
        low = lax.bitwise_and(example_v[p], 127)
        low_hot[:, pl.ds(at, 128)] = (lax.broadcasted_iota(jnp.int32, (128, 128), 0) == low).astype(F32).astype(BF16)

    own_value.wait()
    own_index.wait()
    wait_for(got_index.at[pl.ds(0, ND - 1)], index_sem)
    first_half = lax.broadcasted_iota(jnp.int32, (1, 128), 1) < CAP

    def merged(ref, p):
        return jnp.where(first_half, ref[2 * p], ref[2 * p + 1])

    def flipped(row):
        return pltpu.roll(jnp.broadcast_to(row, (8, 128)), CAP, axis=1)[0:1]

    def logits_of(j):
        blk_from = lax.rem(blk + B - j, B)
        base = blk_from * R
        for h in range(R // 4):
            four = got_values[pl.ds(base + 4 * h, 4)].reshape(4 * CAP, W)
            score = mm_nt(weight_pair[...], jnp.concatenate([four, four], axis=1))
            p = blk_from * X + 2 * h
            for q in range(2):
                name = merged(got_index, p + q)
                hit = lax.broadcasted_iota(jnp.int32, (BD, 128), 0) == name
                row = jnp.sum(jnp.where(hit, score[:, q * 128:(q + 1) * 128], 0.0), axis=0, keepdims=True)
                logit_send[0, p + q] = row
                logit_send[1, p + q] = flipped(row)

        def back(r, _):
            rep_to = lax.rem(rep + r, R)
            to = base + rep_to
            send(logit_send.at[lax.rem(rep_to + core, 2), to // 2], logit_got.at[me], 2, logit_sem, (blk_from, rep_to))
            return 0

        return back

    wait_for(got_values.at[pl.ds(0, R - 1)], value_sem.at[0])
    lax.fori_loop(1, R, logits_of(0), 0)
    logit_got[me] = logit_send[0, me // 2]

    @pl.loop(1, B)
    def _(j):
        wait_for(got_values.at[pl.ds(0, R)], value_sem.at[j])
        lax.fori_loop(0, R, logits_of(j), 0)

    wait_for(logit_got.at[pl.ds(0, ND - 1)], logit_sem)
    eight = lax.broadcasted_iota(jnp.int32, (NH, 128), 0)

    @pl.loop(0, NP)
    def _(p):
        at = pl.multiple_of(p * 128, 128)
        mine = eight == lax.shift_right_logical(example_v[p], 7)
        term = jnp.where(mine, merged(logit_got, p), 0.0)
        top = term.astype(BF16).astype(F32)
        spread[:, pl.ds(at, 128)] = jnp.concatenate([top, term - top], axis=0).astype(BF16)

    wide = mm_nt(spread[...], low_hot[...])
    prob = jax.nn.sigmoid(wide[:NH] + wide[NH:] + deep_v[...])
    prob_o[...] = prob
    residual = prob - labels_v[...].astype(F32)
    dlogit = residual.astype(BF16).astype(F32)

    table = jnp.concatenate([dlogit, jnp.zeros_like(dlogit)], axis=0).astype(BF16)
    picked[...] = mm(table, low_hot[...])

    @pl.loop(0, NP)
    def _(p):
        at = pl.multiple_of(p * 128, 128)
        mine = eight == lax.shift_right_logical(example_v[p], 7)
        row = jnp.sum(jnp.where(mine, picked[0:NH, pl.ds(at, 128)], 0.0), axis=0, keepdims=True)
        res_send[0, p] = row
        res_send[1, p] = flipped(row)

    @pl.loop(1, ND)
    def _(k):
        blk_to = lax.rem(blk + k // R, B)
        rep_to = lax.rem(rep + lax.rem(k, R), R)
        to = blk_to * R + rep_to
        send(res_send.at[lax.rem(rep_to + core, 2), to // 2], res_got.at[me], 3, res_sem, (blk_to, rep_to))

    res_got[me] = res_send[0, me // 2]

    upright = jnp.concatenate([dlogit, jnp.zeros((128 - NH, 128), F32)], axis=0).T
    grad_head = jnp.zeros((8, H2), F32)
    for q in range(NH):
        span = slice(q * 128, (q + 1) * 128)
        column = upright[:, q:q + 1]
        d_two_v[span, :] = (scale_two[span, :] * column).astype(BF16)
        d_one_v[span, :] = (scale_one[span, :] * column).astype(BF16)
        grad_head += mm(jnp.broadcast_to(dlogit[q:q + 1, :], (8, 128)).astype(BF16), hid_two_v[span, :])
    ones = jnp.ones((8, E), BF16)
    bias_one = mm(ones, d_one_v[...])
    bias_two = mm(ones, d_two_v[...])
    small_v[...] = jnp.zeros_like(small_v)
    for q in range(j1):
        small_v[q:q + 1, :] = bias_one[0:1, q * 128:(q + 1) * 128]
    for q in range(j2):
        small_v[j1 + q:j1 + q + 1, :] = bias_two[0:1, q * 128:(q + 1) * 128]
        small_v[j1 + j2 + q:j1 + j2 + q + 1, :] = grad_head[0:1, q * 128:(q + 1) * 128]

    half_one, half_two = DIN // 2, H1 // 2
    theirs_one = pl.multiple_of(other * half_one, half_one)
    theirs_two = pl.multiple_of(other * half_two, half_two)
    mine_one = pl.multiple_of(core * half_one, half_one)
    mine_two = pl.multiple_of(core * half_two, half_two)
    rep_other = rep + 1 - 2 * core
    part_one[...] = mm(dense_t[pl.ds(theirs_one, half_one), :], d_one_v[...]).astype(BF16)
    send(part_one, pair_one, 4, pair_sem.at[0], (blk, rep_other))
    part_two[...] = mm(hid_one_t[pl.ds(theirs_two, half_two), :], d_two_v[...])
    send(part_two, pair_two, 5, pair_sem.at[1], (blk, rep_other))

    @pl.loop(1, R)
    def _(r):
        send(small_v, small_rep.at[rep], 6, small_sem.at[0], (blk, lax.rem(rep + r, R)))

    small_rep[rep] = small_v[...]

    own_one[...] = mm(dense_t[pl.ds(mine_one, half_one), :], d_one_v[...])
    own_two = mm(hid_one_t[pl.ds(mine_two, half_two), :], d_two_v[...])
    wait_for(pair_one, pair_sem.at[0])
    sum_one[...] = (own_one[...] + pair_one[...].astype(F32)).astype(BF16)
    wait_for(pair_two, pair_sem.at[1])
    sum_two[...] = own_two + pair_two[...]

    def piece_one(ref, q, base):
        row = pl.multiple_of(base + (q // j1) * c1, c1)
        return ref.at[pl.ds(row, c1), pl.ds(pl.multiple_of(lax.rem(q, j1) * 128, 128), 128)]

    def piece_two(ref, q, base):
        row = pl.multiple_of(base + (q // j2) * c2, c2)
        return ref.at[pl.ds(row, c2), pl.ds(pl.multiple_of(lax.rem(q, j2) * 128, 128), 128)]

    @pl.loop(1, NC)
    def _(k):
        blk_to = lax.rem(blk + k // X, B)
        x_to = lax.rem(rep // 2 + lax.rem(k, X), X)
        q = blk_to * X + x_to
        where = (blk_to, x_to * 2 + core)
        send(piece_one(sum_one, q, 0), got_one.at[chip], 7, rs_sem.at[0], where)
        send(piece_two(sum_two, q, 0), got_two.at[chip], 8, rs_sem.at[1], where)

    own_a = pltpu.make_async_copy(piece_one(sum_one, chip, 0), got_one.at[chip], own_sem.at[2])
    own_a.start()
    own_b = pltpu.make_async_copy(piece_two(sum_two, chip, 0), got_two.at[chip], own_sem.at[3])
    own_b.start()

    wait_for(res_got.at[pl.ds(0, ND - 1)], res_sem)
    total[...] = jnp.zeros_like(total)

    @pl.loop(0, B)
    def _(g):
        for h in range(X):
            p = g * X + h
            hit = lax.broadcasted_iota(jnp.int32, (BD, 128), 0) == merged(got_index, p)
            block_hot[:, h * 128:(h + 1) * 128] = jnp.where(hit, merged(res_got, p), 0.0).astype(BF16)
        values = got_values[pl.ds(g * R, R)].reshape(R * CAP, W)
        total[...] += mm(block_hot[...], values)

    wait_for(small_rep.at[pl.ds(0, R - 1)], small_sem.at[0])
    acc = small_rep[0]
    for r in range(1, R):
        acc = acc + small_rep[r]
    small_sum[...] = acc

    @pl.loop(1, B)
    def _(k):
        send(small_sum, small_blk.at[blk], 9, small_sem.at[1], (lax.rem(blk + k, B), rep))

    small_blk[blk] = acc
    own_a.wait()
    own_b.wait()
    wait_for(got_one.at[pl.ds(0, NC - 1)], rs_sem.at[0])
    wait_for(got_two.at[pl.ds(0, NC - 1)], rs_sem.at[1])
    fin_one[...] = lax.fori_loop(
        1, NC, lambda q, a: a + got_one[q].astype(F32), got_one[0].astype(F32)
    ).astype(BF16)
    fin_two[...] = lax.fori_loop(1, NC, lambda q, a: a + got_two[q], got_two[0])

    @pl.loop(1, NC)
    def _(k):
        blk_to = lax.rem(blk + k // X, B)
        where = (blk_to, lax.rem(rep // 2 + lax.rem(k, X), X) * 2 + core)
        send(fin_one, piece_one(full_one, chip, mine_one), 10, ag_sem.at[0, k // X], where)
        send(fin_two, piece_two(full_two, chip, mine_two), 11, ag_sem.at[1, k // X], where)

    own_c = pltpu.make_async_copy(fin_one, piece_one(full_one, chip, mine_one), own_sem.at[4])
    own_c.start()
    own_d = pltpu.make_async_copy(fin_two, piece_two(full_two, chip, mine_two), own_sem.at[5])
    own_d.start()

    grad = total[...]
    n_old = n_v[...]
    n_new = n_old + grad * grad
    n_out_v[...] = n_new
    z_out_v[...] = z_v[...] + grad - (jnp.sqrt(n_new) - jnp.sqrt(n_old)) / 0.5 * weight_v[...]
    out_z = pltpu.make_async_copy(z_out_v, z_o, out_sem.at[0])
    out_z.start()
    out_n = pltpu.make_async_copy(n_out_v, n_o, out_sem.at[1])
    out_n.start()

    own_c.wait()
    own_d.wait()
    rows_one, rows_two = X // j1 * c1, X // j2 * c2

    def stripe_one(j, base):
        at = pl.multiple_of(base + lax.rem(blk + B - j, B) * rows_one, rows_one)
        return full_one.at[pl.ds(at, rows_one), :]

    def stripe_two(j, base):
        at = pl.multiple_of(base + lax.rem(blk + B - j, B) * rows_two, rows_two)
        return full_two.at[pl.ds(at, rows_two), :]

    def forward(j):
        send(stripe_one(j, mine_one), stripe_one(j, mine_one), 12, fw_sem.at[0], (blk, rep_other))
        send(stripe_two(j, mine_two), stripe_two(j, mine_two), 13, fw_sem.at[1], (blk, rep_other))

    wait_for(got_one.at[pl.ds(0, X - 1)], ag_sem.at[0, 0])
    wait_for(got_two.at[pl.ds(0, X - 1)], ag_sem.at[1, 0])
    forward(0)

    @pl.loop(1, B)
    def _(j):
        wait_for(got_one.at[pl.ds(0, X)], ag_sem.at[0, j])
        wait_for(got_two.at[pl.ds(0, X)], ag_sem.at[1, j])
        forward(j)

    out_a = pltpu.make_async_copy(full_one.at[pl.ds(mine_one, half_one)], g_one_o.at[pl.ds(mine_one, half_one)], out_sem.at[2])
    out_a.start()
    out_b = pltpu.make_async_copy(full_two.at[pl.ds(mine_two, half_two)], g_two_o.at[pl.ds(mine_two, half_two)], out_sem.at[3])
    out_b.start()

    wait_for(small_blk.at[pl.ds(0, B - 1)], small_sem.at[1])
    acc = small_blk[0]
    for r in range(1, B):
        acc = acc + small_blk[r]
    small_o[...] = acc

    wait_for(full_one.at[pl.ds(0, half_one)], fw_sem.at[0])
    wait_for(full_two.at[pl.ds(0, half_two)], fw_sem.at[1])
    out_c = pltpu.make_async_copy(full_one.at[pl.ds(theirs_one, half_one)], g_one_o.at[pl.ds(theirs_one, half_one)], out_sem.at[4])
    out_c.start()
    out_d = pltpu.make_async_copy(full_two.at[pl.ds(theirs_two, half_two)], g_two_o.at[pl.ds(theirs_two, half_two)], out_sem.at[5])
    out_d.start()
    for copy in (out_z, out_n, out_a, out_b, out_c, out_d):
        copy.wait()

    wait_for(got_index.at[pl.ds(0, ND - 1)], send_sem.at[0])
    wait_for(got_values.at[pl.ds(0, ND - 1)], send_sem.at[1])
    wait_for(logit_got.at[pl.ds(0, ND - 1)], send_sem.at[2])
    wait_for(res_got.at[pl.ds(0, ND - 1)], send_sem.at[3])
    wait_for(part_one, send_sem.at[4])
    wait_for(part_two, send_sem.at[5])
    wait_for(small_rep.at[pl.ds(0, R - 1)], send_sem.at[6])
    wait_for(got_one.at[pl.ds(0, NC - 1)], send_sem.at[7])
    wait_for(got_two.at[pl.ds(0, NC - 1)], send_sem.at[8])
    wait_for(small_blk.at[pl.ds(0, B - 1)], send_sem.at[9])
    wait_for(got_one.at[pl.ds(0, NC - 1)], send_sem.at[10])
    wait_for(got_two.at[pl.ds(0, NC - 1)], send_sem.at[11])
    wait_for(full_one.at[pl.ds(0, half_one)], send_sem.at[12])
    wait_for(full_two.at[pl.ds(0, half_two)], send_sem.at[13])


def solution(mesh):
    B, R = mesh.shape["blk"], mesh.shape["rep"]
    ND = B * R
    NC = ND // 2

    def per_device(
        dense, labels, tile_values, tile_block, tile_example, tile_count, z_state, n_state,
        w_one, b_one, w_two, b_two, head,
    ):
        E, DIN = dense.shape
        _, CAP, W = tile_values.shape
        BD = z_state.shape[0]
        H1, H2 = w_two.shape
        NH = E // 128
        NP = ND // 2
        c1 = DIN * H1 // (128 * ND)
        c2 = H1 * H2 // (128 * ND)
        live = jnp.arange(CAP, dtype=jnp.int32)[None, :] < tile_count[:, None]
        named = jnp.where(live, tile_block, -1)
        index = jnp.concatenate([named, named], axis=1).reshape(ND, 1, 2 * CAP)
        example = tile_example.reshape(NP, 1, 128)
        hbm = pl.BlockSpec(memory_space=pl.ANY)
        vmem = pl.BlockSpec(memory_space=pltpu.VMEM)

        def V(shape, kind=F32):
            return pltpu.VMEM(shape, kind)

        dma = pltpu.SemaphoreType.DMA
        scratch = [
            V((E, DIN), BF16), V((NH, 128), jnp.int32), V((NP, 1, 128), jnp.int32), V((BD, W)), V((BD, W)),
            V((DIN, H1), BF16), V((1, H1)), V((H1, H2), BF16), V((1, H2)), V((1, H2), BF16),
            V((ND, CAP, W), BF16), V((ND, 1, 128), jnp.int32), V((BD, W)), V((BD, 2 * W), BF16),
            V((E, H2), BF16), V((DIN, E), BF16), V((H1, E), BF16), V((E, H1)), V((E, H2)),
            V((NH, 128)), V((128, ND * CAP), BF16),
            V((2, NP, 1, 128)), V((ND, 1, 128)), V((2 * NH, ND * CAP), BF16), V((2 * NH, ND * CAP)),
            V((2, NP, 1, 128)), V((ND, 1, 128)),
            V((BD, R * CAP), BF16), V((BD, W)), V((BD, W)), V((BD, W)),
            V((E, H1), BF16), V((E, H2), BF16),
            V((DIN // 2, H1), BF16), V((H1 // 2, H2)), V((DIN // 2, H1)), V((DIN // 2, H1), BF16), V((H1 // 2, H2)),
            V((DIN // 2, H1), BF16), V((H1 // 2, H2)), V((NC, c1, 128), BF16), V((NC, c2, 128)),
            V((c1, 128), BF16), V((c2, 128)), V((DIN, H1), BF16), V((H1, H2)),
            V((8, 128)), V((R, 8, 128)), V((8, 128)), V((B, 8, 128)),
            dma((10,)), dma((6,)), dma(()), dma((B,)), dma(()), dma(()),
            dma((2,)), dma((2,)), dma((2, B)), dma((2,)), dma((2,)),
            dma((14,)), dma((6,)),
        ]
        shape = jax.ShapeDtypeStruct
        prob, z_new, n_new, g_one, g_two, small = pl.pallas_call(
            functools.partial(step_kernel, B, R),
            out_shape=(
                shape((NH, 128), F32), shape((BD, W), F32), shape((BD, W), F32),
                shape((DIN, H1), BF16), shape((H1, H2), F32), shape((8, 128), F32),
            ),
            in_specs=[hbm] * 12,
            out_specs=(vmem, hbm, hbm, hbm, hbm, vmem),
            scratch_shapes=scratch,
            compiler_params=pltpu.CompilerParams(
                collective_id=0, has_side_effects=True, vmem_limit_bytes=60 * 1024 * 1024
            ),
        )(
            dense, labels.reshape(NH, 128), tile_values, index, example, z_state, n_state,
            w_one, b_one.reshape(1, H1), w_two, b_two.reshape(1, H2), head.reshape(1, H2),
        )
        flat = small.reshape(-1)
        return (
            prob.reshape(E), z_new, n_new, g_one.astype(F32), flat[:H1], g_two,
            flat[H1:H1 + H2], flat[H1 + H2:H1 + 2 * H2],
        )

    every = ("blk", "rep")
    return jax.shard_map(
        per_device,
        mesh=mesh,
        in_specs=(
            P(every, None), P(every), P(every, None, None), P(every, None), P(every, None), P(every),
            P(every, None), P(every, None), P(), P(), P(), P(), P(),
        ),
        out_specs=(P(every), P(every, None), P(every, None), P(), P(), P(), P(), P()),
        check_vma=False,
    )
```

time: 374 us -> 114 us (0.30)
  other arithmetic: 127 us -> 4.38 us
  Pallas kernels: 0 us -> 99.5 us
  blocking collectives: 67.4 us -> 0 us
  local copies, waits for them, and re-layouts: 69 us -> 9.22 us
  waiting for transfers between devices: 50.3 us -> 0 us
  starting transfers between devices: 35.3 us -> 0 us
  between operations: 14.3 us -> 0.68 us
  matrix products: 10.7 us -> 0 us
    scatter-add x2 -> x0, other arithmetic: 102 us -> none  [the longest x1 57 us: per_device(): jnp.zeros((dense.shape[0],), jnp.float32).at[flat_example]]
    pallas_call x0 -> x1, Pallas kernels: none -> 99.5 us  [per_device(): pl.pallas_call(functools.partial(step_kernel, B, R), out_shape=(shape((NH...]
    psum x1 -> x0, blocking collectives: 67.4 us -> none  [per_device(): lax.psum((grad_head, grad_w_two, grad_b_two, grad_w_one, grad_b_one), ('b...]
    gather x3 -> x0, local copies, waits for them, and re-layouts: 60.7 us -> none  [the longest x2 32.9 us: per_device(): tile_residual = jnp.take(residual, flat_example).reshape(owners, capacity)]
    psum x1 -> x0, waiting for transfers between devices: 39.5 us -> none  [per_device(): lax.psum((grad_head, grad_w_two, grad_b_two, grad_w_one, grad_b_one), ('b...]
    all_to_all x4 -> x0, starting transfers between devices: 35.2 us -> none  [the longest x1 11.5 us: per_device(): lax.all_to_all(tile_block, ('blk', 'rep'), split_axis=0, concat_axis=0, t...]
    dot_general x7 -> x0, matrix products: 10.7 us -> none  [the longest x1 2.79 us: per_device(): pre_one = jnp.dot(dense, w_one, preferred_element_type=jnp.float32) + b_one]
    all_to_all x4 -> x0, waiting for transfers between devices: 10.3 us -> none  [the longest x1 9.38 us: per_device(): lax.all_to_all(tile_logit, ('blk', 'rep'), split_axis=0, concat_axis=0, t...]
  transfers between devices with their start and end apart: 5 -> 0, of which waited for: 3 -> 0; matrix products, arithmetic and copies ran while one was open for 25% -> 0% of each run, Pallas kernels for 0% -> 0%
where the time goes in v1:
time: 114 us
  Pallas kernels  99.5 us (87%)
  local copies, waits for them, and re-layouts  9.22 us (8%)
  other arithmetic  4.38 us (4%)
    pallas_call x1, Pallas kernels, per_device(): pl.pallas_call(functools.partial(step_kernel, B, R), out_shape=(shape((NH...  99.5 us
    unnamed x14, local copies, waits for them, and re-layouts  4.68 us
    convert_element_type x1, other arithmetic, per_device(): g_one.astype(F32)  2.92 us

profile of v1, /device:TPU:1, one launch (start us, length us, event | category | flops | bytes accessed | tf_op | source)
XLA Modules:
  0.0 113.8 jit_solution(12334855418518036491)
XLA Ops:
  0.6 1.2 %reshape.47.head_h = bf16[1,256]{1,0:T(2,128)(2,1)} reshape(bf16[256]{0:T(256)(128)(2,1)} %param.25) | data formatting | bytes 1024 | tf_op jit(solution)/shard_map/reshape | solution.py:469
  1.9 0.8 copy.23
  2.7 0.7 fusion
  3.5 0.7 pad_add_fusion
  4.2 0.8 copy.24
  5.0 0.7 reshape.44
  5.7 99.5 %shard_map.188 = (f32[8,128]{1,0:T(8,128)}, f32[1024,128]{1,0:T(8,128)}, f32[1024,128]{1,0:T(8,128)}, bf16[1024,512]{1,0:T(8,128)(2,1)}, f32[512,256]{1,0:T(8,128)}, /*index=5*/f32[8,128]{1,0:T(8,128)}) custom-call(bf16[1024,1024]{1,0:T(8,128)(2,1)} %dense_h.1, s32[8,128]{1,0:T(8,128)} %bitcast.14, bf16[128,64,128]{2,1,0:T(8,128)(2,1)} %values_h.1, ...), custom_call_target="tpu_custom_call" | custom-call | tf_op jit(solution)/shard_map/pallas_call | solution.py:455
  105.2 0.0 copy-start.3
  105.2 0.0 copy-start.2
  105.2 1.3 %slice_bitcast_fusion = f32[512]{0:T(512)} fusion(f32[8,128]{1,0:T(8,128)} %get-tuple-element.18), kind=kLoop, calls=%fused_computation.3 | loop fusion | bytes 4096 | tf_op jit(solution)/shard_map/slice | solution.py:473
  106.5 1.3 %slice_bitcast_fusion.1 = (f32[256]{0:T(256)}, f32[256]{0:T(256)}) fusion(f32[8,128]{1,0:T(8,128)} %get-tuple-element.18), kind=kLoop, calls=%fused_computation.4 | loop fusion | bytes 4096 | tf_op jit(solution)/shard_map/slice | solution.py:474
  107.8 0.0 copy-start.1
  107.8 0.0 copy-start
  107.8 2.9 %convert_element_type.3 = f32[1024,512]{1,0:T(8,128)} convert(bf16[1024,512]{1,0:T(8,128)(2,1)} %get-tuple-element.17) | non-fusion elementwise | flops 524288 | bytes 3145728 | tf_op jit(solution)/shard_map/convert_element_type | solution.py:473
  110.8 0.0 copy-done.3
  110.8 0.6 copy.30
  111.4 0.0 copy-done.2
  111.4 0.8 copy.31
  112.2 0.0 copy-done.1
  112.2 0.8 copy.32
  113.0 0.0 copy-done
  113.0 0.8 copy.33
Async XLA Ops:
  105.2 5.6 %copy-start.3 = (f32[8,128]{1,0:T(8,128)S(1)}, f32[8,128]{1,0:T(8,128)}, u32[]{:S(2)}) copy-start(f32[8,128]{1,0:T(8,128)} %get-tuple-element.14) | copy-start | bytes 12292
  105.2 6.2 %copy-start.2 = (f32[1024,128]{1,0:T(8,128)S(1)}, f32[1024,128]{1,0:T(8,128)}, u32[]{:S(2)}) copy-start(f32[1024,128]{1,0:T(8,128)} %get-tuple-element.31) | copy-start | bytes 1572868
  107.8 4.3 %copy-start.1 = (f32[1024,128]{1,0:T(8,128)S(1)}, f32[1024,128]{1,0:T(8,128)}, u32[]{:S(2)}) copy-start(f32[1024,128]{1,0:T(8,128)} %get-tuple-element.32) | copy-start | bytes 1572868
  107.8 5.1 %copy-start = (f32[512,256]{1,0:T(8,128)S(1)}, f32[512,256]{1,0:T(8,128)}, u32[]{:S(2)}) copy-start(f32[512,256]{1,0:T(8,128)} %get-tuple-element.35) | copy-start | bytes 1572868

commit v2 on v1

v2 whole, which is shorter than its diff:
```python
import functools

import jax
import jax.numpy as jnp
from jax import lax
from jax.experimental import pallas as pl
from jax.experimental.pallas import tpu as pltpu
from jax.sharding import PartitionSpec as P

MESH = pl.DeviceIdType.MESH
F32 = jnp.float32
BF16 = jnp.bfloat16
NT = (((1,), (1,)), ((), ()))
STRIDE = 27


def mm(a, b):
    return jnp.dot(a, b, preferred_element_type=F32)


def mm_nt(a, b):
    return lax.dot_general(a, b, NT, preferred_element_type=F32)


def step_kernel(
    B, R,
    dense_h, labels_h, values_h, block_h, example_h, count_h, z_h, n_h,
    w_one_h, b_one_h, w_two_h, b_two_h, head_h,
    prob_o, z_o, n_o, grads_o, small_o,
    dense_v, labels_v, block_v, example_t, count_v, z_v, n_v, w_one_v, b_one_v, w_two_v, b_two_v, head_v,
    table_v, index_send, example_v,
    got_values, got_index, weight_v, weight_pair,
    hid_two_v, dense_t, hid_one_t, scale_one, scale_two, deep_v, low_hot, slot_hot,
    logit_send, logit_got, spread, picked, res_send, res_got,
    block_hot, total, z_out_v, n_out_v,
    d_one_v, d_two_v, own_one, own_two,
    part, pair, summed, got, final, full,
    small_v, small_rep, small_sum, small_blk,
    load_sem, own_sem, ready_sem, index_sem, value_sem, logit_sem, res_sem,
    pair_sem, rs_sem, ag_sem, fw_sem, small_sem,
    send_sem, out_sem,
):
    ND = B * R
    NC = ND // 2
    X = R // 2
    Z = 4 if B % 4 == 0 else B
    Y = B // Z
    E, DIN = dense_v.shape
    H1 = w_one_v.shape[1]
    H2 = w_two_v.shape[1]
    CAP, W = got_values.shape[1], got_values.shape[2]
    BD = z_v.shape[0]
    NH = E // 128
    NP = ND // 2
    c1 = DIN * H1 // (128 * ND)
    c2 = H1 * H2 // (128 * ND)
    j1 = H1 // 128
    j2 = H2 // 128
    blk = lax.axis_index("blk")
    rep = lax.axis_index("rep")
    y, zz = lax.div(blk, Z), lax.rem(blk, Z)
    x, core = lax.div(rep, 2), lax.rem(rep, 2)
    other = 1 - core
    me = blk * R + rep
    chip = blk * X + x
    y_at = [lax.rem(y + i, Y) * Z for i in range(Y)]
    z_at = [lax.rem(zz + i, Z) for i in range(Z)]
    x_at = [lax.rem(x + i, X) for i in range(X)]

    def chip_at(m):
        spot = (m * STRIDE) % NC
        dy, dz, dx = spot // (Z * X), spot // X % Z, spot % X
        return y_at[dy] + z_at[dz], x_at[dx]

    def chip_from(m):
        spot = lax.rem(m * STRIDE, NC)
        dy, dz, dx = lax.div(spot, Z * X), lax.rem(lax.div(spot, X), Z), lax.rem(spot, X)
        return lax.rem(y + Y - dy, Y) * Z + lax.rem(zz + Z - dz, Z), lax.rem(x + X - dx, X)

    loads = [
        (block_h, block_v), (count_h, count_v), (example_h, example_t), (z_h, z_v), (n_h, n_v), (dense_h, dense_v),
        (w_one_h, w_one_v), (b_one_h, b_one_v), (w_two_h, w_two_v), (b_two_h, b_two_v), (head_h, head_v),
        (labels_h, labels_v),
    ]
    copies = [pltpu.make_async_copy(s, d, load_sem.at[i]) for i, (s, d) in enumerate(loads)]
    for copy in copies:
        copy.start()

    def send(src, dst, sem_at, recv, where):
        pltpu.make_async_remote_copy(
            src_ref=src, dst_ref=dst, send_sem=send_sem.at[sem_at], recv_sem=recv,
            device_id=where, device_id_type=MESH,
        ).start()

    def wait_for(ref, sem):
        pltpu.make_async_copy(ref, ref, sem).wait()

    barrier = pltpu.get_barrier_semaphore()
    for k in range(1, B):
        pl.semaphore_signal(barrier, inc=1, device_id=(lax.rem(blk + k, B), rep), device_id_type=MESH)
    for k in range(1, R):
        pl.semaphore_signal(barrier, inc=1, device_id=(blk, lax.rem(rep + k, R)), device_id_type=MESH)
    own_value = pltpu.make_async_copy(values_h.at[me], got_values.at[me], own_sem.at[0])
    own_value.start()

    first_half = lax.broadcasted_iota(jnp.int32, (1, 128), 1) < CAP
    copies[0].wait()
    copies[1].wait()
    live = lax.broadcasted_iota(jnp.int32, (CAP, ND), 0) < count_v[...]
    named = jnp.where(live, block_v[...], -1).astype(F32)
    table_v[...] = jnp.concatenate([named, named], axis=0).T.astype(jnp.int32)
    for o in range(ND):
        index_send[o] = table_v[o:o + 1, :]

    pl.semaphore_wait(barrier, B + R - 2)
    for k in range(1, R):
        pl.semaphore_signal(ready_sem, inc=1, device_id=(blk, lax.rem(rep + k, R)), device_id_type=MESH)
    copies[2].wait()
    named = example_t[...].astype(F32)
    table_v[...] = jnp.concatenate([named, named], axis=0).T.astype(jnp.int32)
    for p in range(NP):
        example_v[p] = jnp.where(first_half, table_v[2 * p:2 * p + 1, :], table_v[2 * p + 1:2 * p + 2, :])
    pl.semaphore_wait(ready_sem, R - 1)

    for m in range(NC):
        blk_to, x_to = chip_at(m)
        for c in ((1,) if m == 0 else (0, 1)):
            rep_to = x_to * 2 + (other if m == 0 else c)
            to = blk_to * R + rep_to
            send(index_send.at[to], got_index.at[me], 0, index_sem.at[m // 2], (blk_to, rep_to))
            send(values_h.at[to], got_values.at[me], 1, value_sem.at[m // 2], (blk_to, rep_to))
    got_index[me] = index_send[me]

    copies[3].wait()
    copies[4].wait()
    z = z_v[...]
    shrunk = z - jnp.where(z > 0, 0.5, -0.5)
    weight = jnp.where(jnp.abs(z) > 0.5, -shrunk / ((1.0 + jnp.sqrt(n_v[...])) / 0.5 + 0.1), 0.0)
    weight_v[...] = weight
    high = weight.astype(BF16)
    weight_pair[:, :W] = high
    weight_pair[:, W:] = (weight - high.astype(F32)).astype(BF16)

    for copy in copies[5:]:
        copy.wait()
    rows = 256
    head_row = jnp.concatenate([head_v[q:q + 1, :] for q in range(j2)], axis=1)
    head_rows = jnp.broadcast_to(head_row, (8, H2))

    @pl.loop(0, E // rows)
    def _(i):
        at = pl.multiple_of(i * rows, rows)
        dense = dense_v[pl.ds(at, rows), :]
        pre_one = mm(dense, w_one_v[...]) + b_one_v[...]
        gate_one = jax.nn.sigmoid(pre_one)
        hid_one = (pre_one * gate_one).astype(BF16)
        pre_two = mm(hid_one, w_two_v[...]) + b_two_v[...]
        gate_two = jax.nn.sigmoid(pre_two)
        hid_two = (pre_two * gate_two).astype(BF16)
        hid_two_v[pl.ds(at, rows), :] = hid_two
        two = head_row.astype(F32) * (gate_two * (1.0 + pre_two * (1.0 - gate_two)))
        scale_two[pl.ds(at, rows), :] = two
        back = mm_nt(two.astype(BF16), w_two_v[...])
        scale_one[pl.ds(at, rows), :] = back * (gate_one * (1.0 + pre_one * (1.0 - gate_one)))
        deep = mm_nt(head_rows, hid_two)
        for q in range(rows // 128):
            deep_v[pl.ds(i * (rows // 128) + q, 1), :] = deep[0:1, q * 128:(q + 1) * 128]
        dense_t[:, pl.ds(at, rows)] = dense.T
        hid_one_t[:, pl.ds(at, rows)] = hid_one.T

    @pl.loop(0, NP)
    def _(p):
        at = pl.multiple_of(p * 128, 128)
        low = lax.bitwise_and(example_v[p], 127)
        hot = (lax.broadcasted_iota(jnp.int32, (128, 128), 0) == low).astype(F32)
        low_hot[:, pl.ds(at, 128)] = hot.astype(BF16)
        slot_hot[pl.ds(at, 128), :] = hot.T.astype(BF16)

    def merged(ref, p):
        return jnp.where(first_half, ref[2 * p], ref[2 * p + 1])

    def flipped(row):
        return pltpu.roll(jnp.broadcast_to(row, (8, 128)), CAP, axis=1)[0:1]

    def logits_of(places):
        spots = [b * X + xs for b, xs in places]
        four = jnp.concatenate([got_values[pl.ds(2 * q, 2)].reshape(2 * CAP, W) for q in spots], axis=0)
        score = mm_nt(weight_pair[...], jnp.concatenate([four, four], axis=1))
        for i, q in enumerate(spots):
            hit = lax.broadcasted_iota(jnp.int32, (BD, 128), 0) == merged(got_index, q)
            row = jnp.sum(jnp.where(hit, score[:, i * 128:(i + 1) * 128], 0.0), axis=0, keepdims=True)
            logit_send[0, q] = row
            logit_send[1, q] = flipped(row)

    own_value.wait()
    wait_for(got_index.at[pl.ds(0, 3)], index_sem.at[0])
    wait_for(got_values.at[pl.ds(0, 3)], value_sem.at[0])
    b_next, x_next = chip_from(1)
    logits_of([(blk, x), (b_next, x_next)])
    send(logit_send.at[1, chip], logit_got.at[me], 2, logit_sem, (blk, x * 2 + other))
    for c, turn in ((0, core), (1, other)):
        send(logit_send.at[turn, b_next * X + x_next], logit_got.at[me], 2, logit_sem, (b_next, x_next * 2 + c))
    logit_got[me] = logit_send[0, chip]

    @pl.loop(1, NC // 2)
    def _(u):
        wait_for(got_index.at[pl.ds(0, 4)], index_sem.at[u])
        wait_for(got_values.at[pl.ds(0, 4)], value_sem.at[u])
        places = [chip_from(2 * u), chip_from(2 * u + 1)]
        logits_of(places)
        for b_to, x_to in places:
            for c, turn in ((0, core), (1, other)):
                send(logit_send.at[turn, b_to * X + x_to], logit_got.at[me], 2, logit_sem, (b_to, x_to * 2 + c))

    wait_for(logit_got.at[pl.ds(0, ND - 1)], logit_sem)
    eight = lax.broadcasted_iota(jnp.int32, (NH, 128), 0)
    for p in range(NP):
        mine = eight == lax.shift_right_logical(example_v[p], 7)
        term = jnp.where(mine, merged(logit_got, p), 0.0)
        top = term.astype(BF16).astype(F32)
        spread[:, p * 128:(p + 1) * 128] = jnp.concatenate([top, term - top], axis=0).astype(BF16)
    wide = mm(spread[...], slot_hot[...])
    prob = jax.nn.sigmoid(wide[:NH] + wide[NH:] + deep_v[...])
    prob_o[...] = prob
    residual = prob - labels_v[...].astype(F32)
    dlogit = residual.astype(BF16).astype(F32)

    upright = jnp.concatenate([dlogit, jnp.zeros((128 - NH, 128), F32)], axis=0).T
    for q in range(NH):
        span = slice(q * 128, (q + 1) * 128)
        column = upright[:, q:q + 1]
        d_two_v[span, :] = (scale_two[span, :] * column).astype(BF16)
        d_one_v[span, :] = (scale_one[span, :] * column).astype(BF16)

    half_one, half_two = DIN // 2, H1 // 2
    rep_other = x * 2 + other

    def cut_one(q):
        return slice(q // j1 * c1, (q // j1 + 1) * c1), slice(q % j1 * 128, (q % j1 + 1) * 128)

    def cut_two(q):
        return slice(q // j2 * c2, (q // j2 + 1) * c2), slice(q % j2 * 128, (q % j2 + 1) * 128)

    grad_one = mm(dense_t[pl.ds(pl.multiple_of(other * half_one, half_one), half_one), :], d_one_v[...])
    grad_two = mm(hid_one_t[pl.ds(pl.multiple_of(other * half_two, half_two), half_two), :], d_two_v[...])
    for q in range(NC):
        part[q, 0:c1, :] = grad_one[cut_one(q)].astype(BF16)
        part[q, c1:c1 + c2, :] = grad_two[cut_two(q)].astype(BF16)
    send(part, pair, 3, pair_sem, (blk, rep_other))
    own_one[...] = mm(dense_t[pl.ds(pl.multiple_of(core * half_one, half_one), half_one), :], d_one_v[...])
    own_two[...] = mm(hid_one_t[pl.ds(pl.multiple_of(core * half_two, half_two), half_two), :], d_two_v[...])
    wait_for(pair, pair_sem)
    for q in range(NC):
        summed[q, 0:c1, :] = (own_one[cut_one(q)] + pair[q, 0:c1, :].astype(F32)).astype(BF16)
        summed[q, c1:c1 + c2, :] = (own_two[cut_two(q)] + pair[q, c1:c1 + c2, :].astype(F32)).astype(BF16)

    for m in range(1, NC):
        b_to, x_to = chip_at(m)
        send(summed.at[b_to * X + x_to], got.at[chip], 4, rs_sem, (b_to, x_to * 2 + core))
    own_piece = pltpu.make_async_copy(summed.at[chip], got.at[chip], own_sem.at[1])
    own_piece.start()

    table = jnp.concatenate([dlogit, jnp.zeros_like(dlogit)], axis=0).astype(BF16)
    picked[...] = mm(table, low_hot[...])
    for p in range(NP):
        mine = eight == lax.shift_right_logical(example_v[p], 7)
        row = jnp.sum(jnp.where(mine, picked[0:NH, p * 128:(p + 1) * 128], 0.0), axis=0, keepdims=True)
        res_send[0, p] = row
        res_send[1, p] = flipped(row)
    for m in range(NC):
        b_to, x_to = chip_at(m)
        q = b_to * X + x_to
        if m == 0:
            send(res_send.at[1, q], res_got.at[me], 5, res_sem, (b_to, x_to * 2 + other))
        else:
            for c, turn in ((0, core), (1, other)):
                send(res_send.at[turn, q], res_got.at[me], 5, res_sem, (b_to, x_to * 2 + c))
    res_got[me] = res_send[0, chip]

    grad_head = jnp.zeros((8, H2), F32)
    for q in range(NH):
        grad_head += mm(jnp.broadcast_to(dlogit[q:q + 1, :], (8, 128)).astype(BF16), hid_two_v[q * 128:(q + 1) * 128, :])
    ones = jnp.ones((8, E), BF16)
    bias_one = mm(ones, d_one_v[...])
    bias_two = mm(ones, d_two_v[...])
    small_v[...] = jnp.zeros_like(small_v)
    for q in range(j1):
        small_v[q:q + 1, :] = bias_one[0:1, q * 128:(q + 1) * 128]
    for q in range(j2):
        small_v[j1 + q:j1 + q + 1, :] = bias_two[0:1, q * 128:(q + 1) * 128]
        small_v[j1 + j2 + q:j1 + j2 + q + 1, :] = grad_head[0:1, q * 128:(q + 1) * 128]
    for k in range(1, R):
        send(small_v, small_rep.at[rep], 6, small_sem.at[0], (blk, lax.rem(rep + k, R)))
    small_rep[rep] = small_v[...]

    own_piece.wait()
    wait_for(got.at[pl.ds(0, NC - 1)], rs_sem)
    final[...] = lax.fori_loop(
        1, NC, lambda q, a: a + got[q].astype(F32), got[0].astype(F32)
    ).astype(BF16)
    for m in range(1, NC):
        b_to, x_to = chip_at(m)
        send(final, full.at[core, chip], 7, ag_sem.at[m // 4], (b_to, x_to * 2 + core))
    send(final, full.at[core, chip], 8, fw_sem, (blk, rep_other))
    own_final = pltpu.make_async_copy(final, full.at[core, chip], own_sem.at[2])
    own_final.start()

    wait_for(small_rep.at[pl.ds(0, R - 1)], small_sem.at[0])
    acc = small_rep[0]
    for r in range(1, R):
        acc = acc + small_rep[r]
    small_sum[...] = acc
    for k in range(1, B):
        send(small_sum, small_blk.at[blk], 9, small_sem.at[1], (lax.rem(blk + k, B), rep))
    small_blk[blk] = acc

    wait_for(res_got.at[pl.ds(0, ND - 1)], res_sem)
    total[...] = jnp.zeros_like(total)

    @pl.loop(0, B)
    def _(g):
        for h in range(X):
            p = g * X + h
            hit = lax.broadcasted_iota(jnp.int32, (BD, 128), 0) == merged(got_index, p)
            block_hot[:, h * 128:(h + 1) * 128] = jnp.where(hit, merged(res_got, p), 0.0).astype(BF16)
        values = got_values[pl.ds(g * R, R)].reshape(R * CAP, W)
        total[...] += mm(block_hot[...], values)

    grad = total[...]
    n_old = n_v[...]
    n_new = n_old + grad * grad
    n_out_v[...] = n_new
    z_out_v[...] = z_v[...] + grad - (jnp.sqrt(n_new) - jnp.sqrt(n_old)) / 0.5 * weight_v[...]
    out_z = pltpu.make_async_copy(z_out_v, z_o, out_sem.at[0])
    out_z.start()
    out_n = pltpu.make_async_copy(n_out_v, n_o, out_sem.at[1])
    out_n.start()

    own_final.wait()

    def pass_on(m):
        b_from, x_from = chip_from(m)
        q = b_from * X + x_from
        send(full.at[core, q], full.at[core, q], 8, fw_sem, (blk, rep_other))

    wait_for(got.at[pl.ds(0, 3)], ag_sem.at[0])
    for m in range(1, 4):
        pass_on(m)

    @pl.loop(1, NC // 4)
    def _(g):
        wait_for(got.at[pl.ds(0, 4)], ag_sem.at[g])
        for i in range(4):
            pass_on(4 * g + i)

    out_a = pltpu.make_async_copy(full.at[core], grads_o.at[core], out_sem.at[2])
    out_a.start()
    wait_for(small_blk.at[pl.ds(0, B - 1)], small_sem.at[1])
    acc = small_blk[0]
    for r in range(1, B):
        acc = acc + small_blk[r]
    small_o[...] = acc
    wait_for(got, fw_sem)
    out_b = pltpu.make_async_copy(full.at[other], grads_o.at[other], out_sem.at[3])
    out_b.start()

    wait_for(got_index.at[pl.ds(0, ND - 1)], send_sem.at[0])
    wait_for(got_values.at[pl.ds(0, ND - 1)], send_sem.at[1])
    wait_for(logit_got.at[pl.ds(0, ND - 1)], send_sem.at[2])
    wait_for(part, send_sem.at[3])
    wait_for(got.at[pl.ds(0, NC - 1)], send_sem.at[4])
    wait_for(res_got.at[pl.ds(0, ND - 1)], send_sem.at[5])
    wait_for(small_rep.at[pl.ds(0, R - 1)], send_sem.at[6])
    wait_for(got.at[pl.ds(0, NC - 1)], send_sem.at[7])
    wait_for(got, send_sem.at[8])
    wait_for(small_blk.at[pl.ds(0, B - 1)], send_sem.at[9])
    for copy in (out_z, out_n, out_a, out_b):
        copy.wait()


def finish_kernel(
    c1, c2, grads_h, small_h, prob_h, z_h, n_h, prob_o, z_o, n_o, g_one_o, b_one_o, g_two_o, b_two_o, head_o,
    grads_v, z_v, n_v, one_v, two_v, in_sem, out_sem,
):
    NC = grads_v.shape[1]
    DIN, H1 = one_v.shape
    H2 = two_v.shape[1]
    j1, j2 = H1 // 128, H2 // 128
    parts = 2
    step = NC // parts
    ins = [
        pltpu.make_async_copy(grads_h.at[h, pl.ds(i * step, step)], grads_v.at[h, pl.ds(i * step, step)], in_sem.at[h * parts + i])
        for h in range(2) for i in range(parts)
    ]
    in_z = pltpu.make_async_copy(z_h, z_v, in_sem.at[2 * parts])
    in_n = pltpu.make_async_copy(n_h, n_v, in_sem.at[2 * parts + 1])
    for copy in (*ins, in_z, in_n):
        copy.start()
    prob_o[...] = prob_h[...]
    for q in range(j1):
        b_one_o[:, q * 128:(q + 1) * 128] = small_h[q:q + 1, :]
    for q in range(j2):
        b_two_o[:, q * 128:(q + 1) * 128] = small_h[j1 + q:j1 + q + 1, :]
        head_o[:, q * 128:(q + 1) * 128] = small_h[j1 + j2 + q:j1 + j2 + q + 1, :]
    outs = []
    for h in range(2):
        for i in range(parts):
            ins[h * parts + i].wait()
            for q in range(i * step, (i + 1) * step):
                r1 = h * (DIN // 2) + q // j1 * c1
                r2 = h * (H1 // 2) + q // j2 * c2
                one_v[r1:r1 + c1, q % j1 * 128:(q % j1 + 1) * 128] = grads_v[h, q, 0:c1, :].astype(F32)
                two_v[r2:r2 + c2, q % j2 * 128:(q % j2 + 1) * 128] = grads_v[h, q, c1:c1 + c2, :].astype(F32)
            n1, n2 = DIN // (2 * parts), H1 // (2 * parts)
            s1, s2 = (h * parts + i) * n1, (h * parts + i) * n2
            outs.append(pltpu.make_async_copy(one_v.at[pl.ds(s1, n1)], g_one_o.at[pl.ds(s1, n1)], out_sem.at[2 * (h * parts + i)]))
            outs.append(pltpu.make_async_copy(two_v.at[pl.ds(s2, n2)], g_two_o.at[pl.ds(s2, n2)], out_sem.at[2 * (h * parts + i) + 1]))
            outs[-2].start()
            outs[-1].start()
        if h == 0:
            in_z.wait()
            outs.append(pltpu.make_async_copy(z_v, z_o, out_sem.at[4 * parts]))
            outs[-1].start()
            in_n.wait()
            outs.append(pltpu.make_async_copy(n_v, n_o, out_sem.at[4 * parts + 1]))
            outs[-1].start()
    for copy in outs:
        copy.wait()


def solution(mesh):
    B, R = mesh.shape["blk"], mesh.shape["rep"]
    ND = B * R
    NC = ND // 2

    def per_device(
        dense, labels, tile_values, tile_block, tile_example, tile_count, z_state, n_state,
        w_one, b_one, w_two, b_two, head,
    ):
        E, DIN = dense.shape
        _, CAP, W = tile_values.shape
        BD = z_state.shape[0]
        H1, H2 = w_two.shape
        NH = E // 128
        NP = ND // 2
        c1 = DIN * H1 // (128 * ND)
        c2 = H1 * H2 // (128 * ND)
        hbm = pl.BlockSpec(memory_space=pl.ANY)
        vmem = pl.BlockSpec(memory_space=pltpu.VMEM)
        I32 = jnp.int32

        def V(shape, kind=F32):
            return pltpu.VMEM(shape, kind)

        dma = pltpu.SemaphoreType.DMA
        scratch = [
            V((E, DIN), BF16), V((NH, 128), I32), V((CAP, ND), I32), V((CAP, ND), I32), V((1, ND), I32),
            V((BD, W)), V((BD, W)), V((DIN, H1), BF16), V((1, H1)), V((H1, H2), BF16), V((1, H2)), V((H2 // 128, 128), BF16),
            V((ND, 128), I32), V((ND, 1, 128), I32), V((NP, 1, 128), I32),
            V((ND, CAP, W), BF16), V((ND, 1, 128), I32), V((BD, W)), V((BD, 2 * W), BF16),
            V((E, H2), BF16), V((DIN, E), BF16), V((H1, E), BF16), V((E, H1)), V((E, H2)),
            V((NH, 128)), V((128, ND * CAP), BF16), V((ND * CAP, 128), BF16),
            V((2, NP, 1, 128)), V((ND, 1, 128)), V((2 * NH, ND * CAP), BF16), V((2 * NH, ND * CAP)),
            V((2, NP, 1, 128)), V((ND, 1, 128)),
            V((BD, R * CAP), BF16), V((BD, W)), V((BD, W)), V((BD, W)),
            V((E, H1), BF16), V((E, H2), BF16), V((DIN // 2, H1)), V((H1 // 2, H2)),
            V((NC, c1 + c2, 128), BF16), V((NC, c1 + c2, 128), BF16), V((NC, c1 + c2, 128), BF16),
            V((NC, c1 + c2, 128), BF16), V((c1 + c2, 128), BF16), V((2, NC, c1 + c2, 128), BF16),
            V((8, 128)), V((R, 8, 128)), V((8, 128)), V((B, 8, 128)),
            dma((12,)), dma((3,)), pltpu.SemaphoreType.REGULAR, dma((NC // 2,)), dma((NC // 2,)), dma(()), dma(()),
            dma(()), dma(()), dma((NC // 4,)), dma(()), dma((2,)),
            dma((10,)), dma((4,)),
        ]
        shape = jax.ShapeDtypeStruct
        prob, z_new, n_new, grads, small = pl.pallas_call(
            functools.partial(step_kernel, B, R),
            out_shape=(
                shape((NH, 128), F32), shape((BD, W), F32), shape((BD, W), F32),
                shape((2, NC, c1 + c2, 128), BF16), shape((8, 128), F32),
            ),
            in_specs=[hbm] * 13,
            out_specs=(vmem, hbm, hbm, hbm, vmem),
            scratch_shapes=scratch,
            compiler_params=pltpu.CompilerParams(
                collective_id=0, has_side_effects=True, vmem_limit_bytes=60 * 1024 * 1024
            ),
        )(
            dense, labels.reshape(NH, 128), tile_values, tile_block.T, tile_example.T, tile_count.reshape(1, ND),
            z_state, n_state, w_one, b_one.reshape(1, H1), w_two, b_two.reshape(1, H2), head.reshape(H2 // 128, 128),
        )
        prob, z_new, n_new, g_one, g_b_one, g_two, g_b_two, g_head = pl.pallas_call(
            functools.partial(finish_kernel, c1, c2),
            out_shape=(
                shape((NH, 128), F32), shape((BD, W), F32), shape((BD, W), F32), shape((DIN, H1), F32),
                shape((1, H1), F32), shape((H1, H2), F32), shape((1, H2), F32), shape((1, H2), F32),
            ),
            in_specs=[hbm, vmem, vmem, hbm, hbm],
            out_specs=(vmem, hbm, hbm, hbm, vmem, hbm, vmem, vmem),
            scratch_shapes=[
                V((2, NC, c1 + c2, 128), BF16), V((BD, W)), V((BD, W)), V((DIN, H1)), V((H1, H2)), dma((6,)), dma((10,)),
            ],
            compiler_params=pltpu.CompilerParams(vmem_limit_bytes=32 * 1024 * 1024),
        )(grads, small, prob, z_new, n_new)
        return (
            prob.reshape(E), z_new, n_new, g_one, g_b_one.reshape(H1), g_two, g_b_two.reshape(H2), g_head.reshape(H2),
        )

    every = ("blk", "rep")
    return jax.shard_map(
        per_device,
        mesh=mesh,
        in_specs=(
            P(every, None), P(every), P(every, None, None), P(every, None), P(every, None), P(every),
            P(every, None), P(every, None), P(), P(), P(), P(), P(),
        ),
        out_specs=(P(every), P(every, None), P(every, None), P(), P(), P(), P(), P()),
        check_vma=False,
    )
```

time: 114 us -> 84.5 us (0.74)
  Pallas kernels: 99.5 us -> 78.8 us
  local copies, waits for them, and re-layouts: 9.22 us -> 4.75 us
  other arithmetic: 4.38 us -> 0 us
    pallas_call x1, Pallas kernels: 99.5 us -> 75.7 us  [per_device(): pl.pallas_call(functools.partial(step_kernel, B, R), out_shape=(shape((NH...]
    pallas_call x0 -> x1, Pallas kernels: none -> 3.07 us  [per_device(): pl.pallas_call(functools.partial(finish_kernel, c1, c2), out_shape=(shape...]
    convert_element_type x1 -> x0, other arithmetic: 2.92 us -> none  [per_device(): g_one.astype(F32)]
    slice x2 -> x0, local copies, waits for them, and re-layouts: 2.63 us -> none  [the longest x1 1.32 us: per_device(): flat[H1 + H2:H1 + 2 * H2]]
    reshape x2 -> x0, local copies, waits for them, and re-layouts: 1.92 us -> none  [the longest x1 1.22 us: per_device(): head.reshape(1, H2)]
    unnamed x14 -> x10, local copies, waits for them, and re-layouts: 4.68 us -> 4.75 us
where the time goes in v2:
time: 84.5 us; the launch traced here: 84.2 us
  Pallas kernels  78.8 us (93%)
  local copies, waits for them, and re-layouts  4.75 us (6%)
    pallas_call x1, Pallas kernels, per_device(): pl.pallas_call(functools.partial(step_kernel, B, R), out_shape=(shape((NH...  75.7 us
    unnamed x10, local copies, waits for them, and re-layouts  4.75 us
    pallas_call x1, Pallas kernels, per_device(): pl.pallas_call(functools.partial(finish_kernel, c1, c2), out_shape=(shape...  3.07 us

profile of v2, /device:TPU:1, one launch (start us, length us, event | category | flops | bytes accessed | tf_op | source)
XLA Modules:
  0.0 84.2 jit_solution(17491283087060899332)
XLA Ops:
  0.6 75.7 %shard_map.188 = (f32[8,128]{1,0:T(8,128)}, f32[1024,128]{1,0:T(8,128)}, f32[1024,128]{1,0:T(8,128)}, bf16[2,64,40,128]{3,2,1,0:T(8,128)(2,1)}, f32[8,128]{1,0:T(8,128)}) custom-call(bf16[1024,1024]{1,0:T(8,128)(2,1)} %dense_h.1, s32[8,128]{1,0:T(8,128)} %bitcast.13, bf16[128,64,128]{2,1,0:T(8,128)(2,1)} %values_h.1, s32[64,128]{1,0:T(8,128)} %bitcast.11, ...), custom_call_target="tpu_custom_call" | custom-call | tf_op jit(solution)/shard_map/pallas_call | solution.py:475
  76.4 0.0 copy-start
  76.4 1.3 %copy-done = bf16[2,64,40,128]{3,2,1,0:T(8,128)(2,1)S(1)} copy-done((bf16[2,64,40,128]{3,2,1,0:T(8,128)(2,1)S(1)}, bf16[2,64,40,128]{3,2,1,0:T(8,128)(2,1)}, u32[]{:S(2)}) %copy-start) | copy-done | bytes 1310744
  77.7 0.0 copy-start.1
  77.7 1.0 %copy-done.1 = f32[1024,128]{1,0:T(8,128)S(1)} copy-done((f32[1024,128]{1,0:T(8,128)S(1)}, f32[1024,128]{1,0:T(8,128)}, u32[]{:S(2)}) %copy-start.1) | copy-done | bytes 524312
  78.7 0.0 copy-start.2
  78.7 1.0 %copy-done.2 = f32[1024,128]{1,0:T(8,128)S(1)} copy-done((f32[1024,128]{1,0:T(8,128)S(1)}, f32[1024,128]{1,0:T(8,128)}, u32[]{:S(2)}) %copy-start.2) | copy-done | bytes 524312
  79.8 0.0 copy-start.3
  79.8 0.7 copy-done.3
  80.4 0.0 copy-start.4
  80.5 0.7 copy-done.4
  81.1 3.1 %shard_map.189 = (f32[8,128]{1,0:T(8,128)}, f32[1024,128]{1,0:T(8,128)}, f32[1024,128]{1,0:T(8,128)}, f32[1024,512]{1,0:T(8,128)}, f32[1,512]{1,0:T(1,128)}, /*i...) custom-call(bf16[2,64,40,128]{3,2,1,0:T(8,128)(2,1)S(1)} %copy-done, f32[8,128]{1,0:T(8,128)S(1)} %copy-done.4, ...), custom_call_target="tpu_custom_call" | custom-call | tf_op jit(solution)/shard_map/pallas_call | solution.py:491
Async XLA Ops:
  76.4 1.3 %copy-start = (bf16[2,64,40,128]{3,2,1,0:T(8,128)(2,1)S(1)}, bf16[2,64,40,128]{3,2,1,0:T(8,128)(2,1)}, u32[]{:S(2)}) copy-start(bf16[2,64,40,128]{3,2,1,0:T(8,128)(2,1)} %get-tuple-element.21.grads_h) | copy-start | bytes 3932164
  77.7 1.0 %copy-start.1 = (f32[1024,128]{1,0:T(8,128)S(1)}, f32[1024,128]{1,0:T(8,128)}, u32[]{:S(2)}) copy-start(f32[1024,128]{1,0:T(8,128)} %get-tuple-element.24.z_h) | copy-start | bytes 1572868
  78.7 1.0 %copy-start.2 = (f32[1024,128]{1,0:T(8,128)S(1)}, f32[1024,128]{1,0:T(8,128)}, u32[]{:S(2)}) copy-start(f32[1024,128]{1,0:T(8,128)} %get-tuple-element.25.n_h) | copy-start | bytes 1572868
  79.8 0.7 copy-start.3
  80.4 0.7 copy-start.4

commit v3 on v2

--- a/solution.py
+++ b/solution.py
@@ -26,7 +26,7 @@
     B, R,
     dense_h, labels_h, values_h, block_h, example_h, count_h, z_h, n_h,
     w_one_h, b_one_h, w_two_h, b_two_h, head_h,
-    prob_o, z_o, n_o, grads_o, small_o,
+    prob_o, z_o, n_o, grad_a_o, grad_b_o, small_o,
     dense_v, labels_v, block_v, example_t, count_v, z_v, n_v, w_one_v, b_one_v, w_two_v, b_two_v, head_v,
     table_v, index_send, example_v,
     got_values, got_index, weight_v, weight_pair,
@@ -34,7 +34,7 @@
     logit_send, logit_got, spread, picked, res_send, res_got,
     block_hot, total, z_out_v, n_out_v,
     d_one_v, d_two_v, own_one, own_two,
-    part, pair, summed, got, final, full,
+    part_a, pair_a, sum_a, got_a, final_a, full_a, part_b, pair_b, sum_b, got_b, final_b, full_b,
     small_v, small_rep, small_sum, small_blk,
     load_sem, own_sem, ready_sem, index_sem, value_sem, logit_sem, res_sem,
     pair_sem, rs_sem, ag_sem, fw_sem, small_sem,
@@ -115,6 +115,22 @@
     pl.semaphore_wait(barrier, B + R - 2)
     for k in range(1, R):
         pl.semaphore_signal(ready_sem, inc=1, device_id=(blk, lax.rem(rep + k, R)), device_id_type=MESH)
+
+    def give(m, c):
+        blk_to, x_to = chip_at(m)
+        rep_to = x_to * 2 + c
+        to = blk_to * R + rep_to
+        send(index_send.at[to], got_index.at[me], 0, index_sem.at[m // 2], (blk_to, rep_to))
+        send(values_h.at[to], got_values.at[me], 1, value_sem.at[m // 2], (blk_to, rep_to))
+
+    give(0, other)
+    for m in range(1, NC):
+        spot = (m * STRIDE) % NC
+        if spot < X:
+            give(m, 0)
+            give(m, 1)
+        elif spot % X == 0:
+            give(m, core)
     copies[2].wait()
     named = example_t[...].astype(F32)
     table_v[...] = jnp.concatenate([named, named], axis=0).T.astype(jnp.int32)
@@ -122,13 +138,13 @@
         example_v[p] = jnp.where(first_half, table_v[2 * p:2 * p + 1, :], table_v[2 * p + 1:2 * p + 2, :])
     pl.semaphore_wait(ready_sem, R - 1)
 
-    for m in range(NC):
-        blk_to, x_to = chip_at(m)
-        for c in ((1,) if m == 0 else (0, 1)):
-            rep_to = x_to * 2 + (other if m == 0 else c)
-            to = blk_to * R + rep_to
-            send(index_send.at[to], got_index.at[me], 0, index_sem.at[m // 2], (blk_to, rep_to))
-            send(values_h.at[to], got_values.at[me], 1, value_sem.at[m // 2], (blk_to, rep_to))
+    for m in range(1, NC):
+        spot = (m * STRIDE) % NC
+        if spot >= X and spot % X == 0:
+            give(m, other)
+        elif spot >= X:
+            give(m, 0)
+            give(m, 1)
     got_index[me] = index_send[me]
 
     copies[3].wait()
@@ -233,32 +249,51 @@
         d_one_v[span, :] = (scale_one[span, :] * column).astype(BF16)
 
     half_one, half_two = DIN // 2, H1 // 2
+    quarter = DIN // 4
     rep_other = x * 2 + other
-
-    def cut_one(q):
-        return slice(q // j1 * c1, (q // j1 + 1) * c1), slice(q % j1 * 128, (q % j1 + 1) * 128)
-
-    def cut_two(q):
-        return slice(q // j2 * c2, (q // j2 + 1) * c2), slice(q % j2 * 128, (q % j2 + 1) * 128)
-
-    grad_one = mm(dense_t[pl.ds(pl.multiple_of(other * half_one, half_one), half_one), :], d_one_v[...])
-    grad_two = mm(hid_one_t[pl.ds(pl.multiple_of(other * half_two, half_two), half_two), :], d_two_v[...])
+    ca = c1 // 2
+
+    def cut(q, height, across):
+        return slice(q // across * height, (q // across + 1) * height), slice(q % across * 128, (q % across + 1) * 128)
+
+    def grad_one(which, piece):
+        return mm(dense_t[pl.ds(pl.multiple_of(which * half_one + piece * quarter, quarter), quarter), :], d_one_v[...])
+
+    def grad_two(which):
+        return mm(hid_one_t[pl.ds(pl.multiple_of(which * half_two, half_two), half_two), :], d_two_v[...])
+
+    one = grad_one(other, 0)
     for q in range(NC):
-        part[q, 0:c1, :] = grad_one[cut_one(q)].astype(BF16)
-        part[q, c1:c1 + c2, :] = grad_two[cut_two(q)].astype(BF16)
-    send(part, pair, 3, pair_sem, (blk, rep_other))
-    own_one[...] = mm(dense_t[pl.ds(pl.multiple_of(core * half_one, half_one), half_one), :], d_one_v[...])
-    own_two[...] = mm(hid_one_t[pl.ds(pl.multiple_of(core * half_two, half_two), half_two), :], d_two_v[...])
-    wait_for(pair, pair_sem)
+        part_a[q] = one[cut(q, ca, j1)].astype(BF16)
+    send(part_a, pair_a, 3, pair_sem.at[0], (blk, rep_other))
+    one = grad_one(other, 1)
+    two = grad_two(other)
     for q in range(NC):
-        summed[q, 0:c1, :] = (own_one[cut_one(q)] + pair[q, 0:c1, :].astype(F32)).astype(BF16)
-        summed[q, c1:c1 + c2, :] = (own_two[cut_two(q)] + pair[q, c1:c1 + c2, :].astype(F32)).astype(BF16)
-
+        part_b[q, 0:ca, :] = one[cut(q, ca, j1)].astype(BF16)
+        part_b[q, ca:ca + c2, :] = two[cut(q, c2, j2)].astype(BF16)
+    send(part_b, pair_b, 10, pair_sem.at[1], (blk, rep_other))
+
+    own_one[...] = grad_one(core, 0)
+    wait_for(pair_a, pair_sem.at[0])
+    for q in range(NC):
+        sum_a[q] = (own_one[cut(q, ca, j1)] + pair_a[q].astype(F32)).astype(BF16)
     for m in range(1, NC):
         b_to, x_to = chip_at(m)
-        send(summed.at[b_to * X + x_to], got.at[chip], 4, rs_sem, (b_to, x_to * 2 + core))
-    own_piece = pltpu.make_async_copy(summed.at[chip], got.at[chip], own_sem.at[1])
-    own_piece.start()
+        send(sum_a.at[b_to * X + x_to], got_a.at[chip], 4, rs_sem.at[0], (b_to, x_to * 2 + core))
+    own_a = pltpu.make_async_copy(sum_a.at[chip], got_a.at[chip], own_sem.at[1])
+    own_a.start()
+
+    own_one[...] = grad_one(core, 1)
+    own_two[...] = grad_two(core)
+    wait_for(pair_b, pair_sem.at[1])
+    for q in range(NC):
+        sum_b[q, 0:ca, :] = (own_one[cut(q, ca, j1)] + pair_b[q, 0:ca, :].astype(F32)).astype(BF16)
+        sum_b[q, ca:ca + c2, :] = (own_two[cut(q, c2, j2)] + pair_b[q, ca:ca + c2, :].astype(F32)).astype(BF16)
+    for m in range(1, NC):
+        b_to, x_to = chip_at(m)
+        send(sum_b.at[b_to * X + x_to], got_b.at[chip], 11, rs_sem.at[1], (b_to, x_to * 2 + core))
+    own_b = pltpu.make_async_copy(sum_b.at[chip], got_b.at[chip], own_sem.at[2])
+    own_b.start()
 
     table = jnp.concatenate([dlogit, jnp.zeros_like(dlogit)], axis=0).astype(BF16)
     picked[...] = mm(table, low_hot[...])
@@ -293,17 +328,22 @@
         send(small_v, small_rep.at[rep], 6, small_sem.at[0], (blk, lax.rem(rep + k, R)))
     small_rep[rep] = small_v[...]
 
-    own_piece.wait()
-    wait_for(got.at[pl.ds(0, NC - 1)], rs_sem)
-    final[...] = lax.fori_loop(
-        1, NC, lambda q, a: a + got[q].astype(F32), got[0].astype(F32)
-    ).astype(BF16)
-    for m in range(1, NC):
-        b_to, x_to = chip_at(m)
-        send(final, full.at[core, chip], 7, ag_sem.at[m // 4], (b_to, x_to * 2 + core))
-    send(final, full.at[core, chip], 8, fw_sem, (blk, rep_other))
-    own_final = pltpu.make_async_copy(final, full.at[core, chip], own_sem.at[2])
-    own_final.start()
+    def hand_out(own, got, final, full, piece, sem_at):
+        own.wait()
+        wait_for(got.at[pl.ds(0, NC - 1)], rs_sem.at[piece])
+        final[...] = lax.fori_loop(
+            1, NC, lambda q, a: a + got[q].astype(F32), got[0].astype(F32)
+        ).astype(BF16)
+        for m in range(1, NC):
+            b_to, x_to = chip_at(m)
+            send(final, full.at[core, chip], sem_at, ag_sem.at[piece, m // 4], (b_to, x_to * 2 + core))
+        send(final, full.at[core, chip], 8 + 5 * piece, fw_sem.at[piece], (blk, rep_other))
+        copy = pltpu.make_async_copy(final, full.at[core, chip], own_sem.at[3 + piece])
+        copy.start()
+        return copy
+
+    own_final_a = hand_out(own_a, got_a, final_a, full_a, 0, 7)
+    own_final_b = hand_out(own_b, got_b, final_b, full_b, 1, 12)
 
     wait_for(small_rep.at[pl.ds(0, R - 1)], small_sem.at[0])
     acc = small_rep[0]
@@ -336,64 +376,76 @@
     out_n = pltpu.make_async_copy(n_out_v, n_o, out_sem.at[1])
     out_n.start()
 
-    own_final.wait()
-
-    def pass_on(m):
-        b_from, x_from = chip_from(m)
-        q = b_from * X + x_from
-        send(full.at[core, q], full.at[core, q], 8, fw_sem, (blk, rep_other))
-
-    wait_for(got.at[pl.ds(0, 3)], ag_sem.at[0])
-    for m in range(1, 4):
-        pass_on(m)
-
-    @pl.loop(1, NC // 4)
-    def _(g):
-        wait_for(got.at[pl.ds(0, 4)], ag_sem.at[g])
-        for i in range(4):
-            pass_on(4 * g + i)
-
-    out_a = pltpu.make_async_copy(full.at[core], grads_o.at[core], out_sem.at[2])
-    out_a.start()
+    def pass_all(own, got, full, out_h, piece):
+        own.wait()
+
+        def pass_on(m):
+            b_from, x_from = chip_from(m)
+            q = b_from * X + x_from
+            send(full.at[core, q], full.at[core, q], 8 + 5 * piece, fw_sem.at[piece], (blk, rep_other))
+
+        wait_for(got.at[pl.ds(0, 3)], ag_sem.at[piece, 0])
+        for m in range(1, 4):
+            pass_on(m)
+
+        @pl.loop(1, NC // 4)
+        def _(g):
+            wait_for(got.at[pl.ds(0, 4)], ag_sem.at[piece, g])
+            for i in range(4):
+                pass_on(4 * g + i)
+
+        copy = pltpu.make_async_copy(full.at[core], out_h.at[core], out_sem.at[2 + piece])
+        copy.start()
+        return copy
+
+    out_a = pass_all(own_final_a, got_a, full_a, grad_a_o, 0)
+    out_b = pass_all(own_final_b, got_b, full_b, grad_b_o, 1)
     wait_for(small_blk.at[pl.ds(0, B - 1)], small_sem.at[1])
     acc = small_blk[0]
     for r in range(1, B):
         acc = acc + small_blk[r]
     small_o[...] = acc
-    wait_for(got, fw_sem)
-    out_b = pltpu.make_async_copy(full.at[other], grads_o.at[other], out_sem.at[3])
-    out_b.start()
+    wait_for(got_a, fw_sem.at[0])
+    out_c = pltpu.make_async_copy(full_a.at[other], grad_a_o.at[other], out_sem.at[4])
+    out_c.start()
+    wait_for(got_b, fw_sem.at[1])
+    out_d = pltpu.make_async_copy(full_b.at[other], grad_b_o.at[other], out_sem.at[5])
+    out_d.start()
 
     wait_for(got_index.at[pl.ds(0, ND - 1)], send_sem.at[0])
     wait_for(got_values.at[pl.ds(0, ND - 1)], send_sem.at[1])
     wait_for(logit_got.at[pl.ds(0, ND - 1)], send_sem.at[2])
-    wait_for(part, send_sem.at[3])
-    wait_for(got.at[pl.ds(0, NC - 1)], send_sem.at[4])
+    wait_for(part_a, send_sem.at[3])
+    wait_for(got_a.at[pl.ds(0, NC - 1)], send_sem.at[4])
     wait_for(res_got.at[pl.ds(0, ND - 1)], send_sem.at[5])
     wait_for(small_rep.at[pl.ds(0, R - 1)], send_sem.at[6])
-    wait_for(got.at[pl.ds(0, NC - 1)], send_sem.at[7])
-    wait_for(got, send_sem.at[8])
+    wait_for(got_a.at[pl.ds(0, NC - 1)], send_sem.at[7])
+    wait_for(got_a, send_sem.at[8])
+    wait_for(part_b, send_sem.at[10])
+    wait_for(got_b.at[pl.ds(0, NC - 1)], send_sem.at[11])
+    wait_for(got_b.at[pl.ds(0, NC - 1)], send_sem.at[12])
+    wait_for(got_b, send_sem.at[13])
     wait_for(small_blk.at[pl.ds(0, B - 1)], send_sem.at[9])
-    for copy in (out_z, out_n, out_a, out_b):
+    for copy in (out_z, out_n, out_a, out_b, out_c, out_d):
         copy.wait()
 
 
 def finish_kernel(
-    c1, c2, grads_h, small_h, prob_h, z_h, n_h, prob_o, z_o, n_o, g_one_o, b_one_o, g_two_o, b_two_o, head_o,
-    grads_v, z_v, n_v, one_v, two_v, in_sem, out_sem,
+    c1, c2, grad_a_h, grad_b_h, small_h, prob_h, z_h, n_h, prob_o, z_o, n_o, g_one_o, b_one_o, g_two_o, b_two_o, head_o,
+    grad_a_v, grad_b_v, z_v, n_v, one_v, two_v, in_sem, out_sem,
 ):
-    NC = grads_v.shape[1]
+    NC = grad_a_v.shape[1]
     DIN, H1 = one_v.shape
     H2 = two_v.shape[1]
     j1, j2 = H1 // 128, H2 // 128
-    parts = 2
-    step = NC // parts
-    ins = [
-        pltpu.make_async_copy(grads_h.at[h, pl.ds(i * step, step)], grads_v.at[h, pl.ds(i * step, step)], in_sem.at[h * parts + i])
-        for h in range(2) for i in range(parts)
-    ]
-    in_z = pltpu.make_async_copy(z_h, z_v, in_sem.at[2 * parts])
-    in_n = pltpu.make_async_copy(n_h, n_v, in_sem.at[2 * parts + 1])
+    ca = c1 // 2
+    quarter = DIN // 4
+    ins = []
+    for h in range(2):
+        ins.append(pltpu.make_async_copy(grad_a_h.at[h], grad_a_v.at[h], in_sem.at[2 * h]))
+        ins.append(pltpu.make_async_copy(grad_b_h.at[h], grad_b_v.at[h], in_sem.at[2 * h + 1]))
+    in_z = pltpu.make_async_copy(z_h, z_v, in_sem.at[4])
+    in_n = pltpu.make_async_copy(n_h, n_v, in_sem.at[5])
     for copy in (*ins, in_z, in_n):
         copy.start()
     prob_o[...] = prob_h[...]
@@ -403,27 +455,29 @@
         b_two_o[:, q * 128:(q + 1) * 128] = small_h[j1 + q:j1 + q + 1, :]
         head_o[:, q * 128:(q + 1) * 128] = small_h[j1 + j2 + q:j1 + j2 + q + 1, :]
     outs = []
+
+    def out(src, dst):
+        outs.append(pltpu.make_async_copy(src, dst, out_sem.at[len(outs)]))
+        outs[-1].start()
+
     for h in range(2):
-        for i in range(parts):
-            ins[h * parts + i].wait()
-            for q in range(i * step, (i + 1) * step):
-                r1 = h * (DIN // 2) + q // j1 * c1
-                r2 = h * (H1 // 2) + q // j2 * c2
-                one_v[r1:r1 + c1, q % j1 * 128:(q % j1 + 1) * 128] = grads_v[h, q, 0:c1, :].astype(F32)
-                two_v[r2:r2 + c2, q % j2 * 128:(q % j2 + 1) * 128] = grads_v[h, q, c1:c1 + c2, :].astype(F32)
-            n1, n2 = DIN // (2 * parts), H1 // (2 * parts)
-            s1, s2 = (h * parts + i) * n1, (h * parts + i) * n2
-            outs.append(pltpu.make_async_copy(one_v.at[pl.ds(s1, n1)], g_one_o.at[pl.ds(s1, n1)], out_sem.at[2 * (h * parts + i)]))
-            outs.append(pltpu.make_async_copy(two_v.at[pl.ds(s2, n2)], g_two_o.at[pl.ds(s2, n2)], out_sem.at[2 * (h * parts + i) + 1]))
-            outs[-2].start()
-            outs[-1].start()
+        for piece, ref in ((0, grad_a_v), (1, grad_b_v)):
+            ins[2 * h + piece].wait()
+            top = h * (DIN // 2) + piece * quarter
+            for q in range(NC):
+                r1 = top + q // j1 * ca
+                one_v[r1:r1 + ca, q % j1 * 128:(q % j1 + 1) * 128] = ref[h, q, 0:ca, :].astype(F32)
+                if piece == 1:
+                    r2 = h * (H1 // 2) + q // j2 * c2
+                    two_v[r2:r2 + c2, q % j2 * 128:(q % j2 + 1) * 128] = ref[h, q, ca:ca + c2, :].astype(F32)
+            out(one_v.at[pl.ds(top, quarter)], g_one_o.at[pl.ds(top, quarter)])
+            if piece == 1:
+                out(two_v.at[pl.ds(h * (H1 // 2), H1 // 2)], g_two_o.at[pl.ds(h * (H1 // 2), H1 // 2)])
         if h == 0:
             in_z.wait()
-            outs.append(pltpu.make_async_copy(z_v, z_o, out_sem.at[4 * parts]))
-            outs[-1].start()
+            out(z_v, z_o)
             in_n.wait()
-            outs.append(pltpu.make_async_copy(n_v, n_o, out_sem.at[4 * parts + 1]))
-            outs[-1].start()
+            out(n_v, n_o)
     for copy in outs:
         copy.wait()
 
@@ -452,6 +506,10 @@
         def V(shape, kind=F32):
             return pltpu.VMEM(shape, kind)
 
+        def slabs(high):
+            each = V((NC, high, 128), BF16)
+            return each, each, each, each, V((high, 128), BF16), V((2, NC, high, 128), BF16)
+
         dma = pltpu.SemaphoreType.DMA
         scratch = [
             V((E, DIN), BF16), V((NH, 128), I32), V((CAP, ND), I32), V((CAP, ND), I32), V((1, ND), I32),
@@ -463,23 +521,22 @@
             V((2, NP, 1, 128)), V((ND, 1, 128)), V((2 * NH, ND * CAP), BF16), V((2 * NH, ND * CAP)),
             V((2, NP, 1, 128)), V((ND, 1, 128)),
             V((BD, R * CAP), BF16), V((BD, W)), V((BD, W)), V((BD, W)),
-            V((E, H1), BF16), V((E, H2), BF16), V((DIN // 2, H1)), V((H1 // 2, H2)),
-            V((NC, c1 + c2, 128), BF16), V((NC, c1 + c2, 128), BF16), V((NC, c1 + c2, 128), BF16),
-            V((NC, c1 + c2, 128), BF16), V((c1 + c2, 128), BF16), V((2, NC, c1 + c2, 128), BF16),
+            V((E, H1), BF16), V((E, H2), BF16), V((DIN // 4, H1)), V((H1 // 2, H2)),
+            *slabs(c1 // 2), *slabs(c1 // 2 + c2),
             V((8, 128)), V((R, 8, 128)), V((8, 128)), V((B, 8, 128)),
-            dma((12,)), dma((3,)), pltpu.SemaphoreType.REGULAR, dma((NC // 2,)), dma((NC // 2,)), dma(()), dma(()),
-            dma(()), dma(()), dma((NC // 4,)), dma(()), dma((2,)),
-            dma((10,)), dma((4,)),
+            dma((12,)), dma((5,)), pltpu.SemaphoreType.REGULAR, dma((NC // 2,)), dma((NC // 2,)), dma(()), dma(()),
+            dma((2,)), dma((2,)), dma((2, NC // 4)), dma((2,)), dma((2,)),
+            dma((14,)), dma((6,)),
         ]
         shape = jax.ShapeDtypeStruct
-        prob, z_new, n_new, grads, small = pl.pallas_call(
+        prob, z_new, n_new, grad_a, grad_b, small = pl.pallas_call(
             functools.partial(step_kernel, B, R),
             out_shape=(
                 shape((NH, 128), F32), shape((BD, W), F32), shape((BD, W), F32),
-                shape((2, NC, c1 + c2, 128), BF16), shape((8, 128), F32),
+                shape((2, NC, c1 // 2, 128), BF16), shape((2, NC, c1 // 2 + c2, 128), BF16), shape((8, 128), F32),
             ),
             in_specs=[hbm] * 13,
-            out_specs=(vmem, hbm, hbm, hbm, vmem),
+            out_specs=(vmem, hbm, hbm, hbm, hbm, vmem),
             scratch_shapes=scratch,
             compiler_params=pltpu.CompilerParams(
                 collective_id=0, has_side_effects=True, vmem_limit_bytes=60 * 1024 * 1024
@@ -494,13 +551,14 @@
                 shape((NH, 128), F32), shape((BD, W), F32), shape((BD, W), F32), shape((DIN, H1), F32),
                 shape((1, H1), F32), shape((H1, H2), F32), shape((1, H2), F32), shape((1, H2), F32),
             ),
-            in_specs=[hbm, vmem, vmem, hbm, hbm],
+            in_specs=[hbm, hbm, vmem, vmem, hbm, hbm],
             out_specs=(vmem, hbm, hbm, hbm, vmem, hbm, vmem, vmem),
             scratch_shapes=[
-                V((2, NC, c1 + c2, 128), BF16), V((BD, W)), V((BD, W)), V((DIN, H1)), V((H1, H2)), dma((6,)), dma((10,)),
+                V((2, NC, c1 // 2, 128), BF16), V((2, NC, c1 // 2 + c2, 128), BF16), V((BD, W)), V((BD, W)),
+                V((DIN, H1)), V((H1, H2)), dma((6,)), dma((8,)),
             ],
-            compiler_params=pltpu.CompilerParams(vmem_limit_bytes=32 * 1024 * 1024),
-        )(grads, small, prob, z_new, n_new)
+            compiler_params=pltpu.CompilerParams(vmem_limit_bytes=63 * 1024 * 1024),
+        )(grad_a, grad_b, small, prob, z_new, n_new)
         return (
             prob.reshape(E), z_new, n_new, g_one, g_b_one.reshape(H1), g_two, g_b_two.reshape(H2), g_head.reshape(H2),
         )

time: 84.5 us -> 79.3 us (0.938)
  local copies, waits for them, and re-layouts: 4.75 us -> 0 us
    unnamed x10 -> x0, local copies, waits for them, and re-layouts: 4.75 us -> none
    pallas_call x1, Pallas kernels: 75.7 us -> 74.2 us  [per_device(): pl.pallas_call(functools.partial(step_kernel, B, R), out_shape=(shape((NH...]
    pallas_call x1, Pallas kernels: 3.07 us -> 4.24 us  [per_device(): pl.pallas_call(functools.partial(finish_kernel, c1, c2), out_shape=(shape...]
where the time goes in v3:
time: 79.3 us; the launch traced here: 79.1 us
  Pallas kernels  78.5 us (99%)
    pallas_call x1, Pallas kernels, per_device(): pl.pallas_call(functools.partial(step_kernel, B, R), out_shape=(shape((NH...  74.2 us
    pallas_call x1, Pallas kernels, per_device(): pl.pallas_call(functools.partial(finish_kernel, c1, c2), out_shape=(shape...  4.24 us

profile of v3, /device:TPU:1, one launch (start us, length us, event | category | flops | bytes accessed | tf_op | source)
XLA Modules:
  0.0 79.1 jit_solution(13126648475612850956)
XLA Ops:
  0.6 74.2 %shard_map.188 = (f32[8,128]{1,0:T(8,128)}, f32[1024,128]{1,0:T(8,128)}, f32[1024,128]{1,0:T(8,128)}, bf16[2,64,16,128]{3,2,1,0:T(8,128)(2,1)}, bf16[2,64,24,128]{3,2,1,0:T(8,128)(2,1)}, /*index=5*/f32[8,128]{1,0:T(8,128)}) custom-call(bf16[1024,1024]{1,0:T(8,128)(2,1)} %dense_h.1, s32[8,128]{1,0:T(8,128)} %bitcast.13, bf16[128,64,128]{2,1,0:T(8,128)(2,1)} %values_h.1, ...), custom_call_target="tpu_custom_call" | custom-call | tf_op jit(solution)/shard_map/pallas_call | solution.py:532
  74.9 4.2 %shard_map.189 = (f32[8,128]{1,0:T(8,128)}, f32[1024,128]{1,0:T(8,128)}, f32[1024,128]{1,0:T(8,128)}, f32[1024,512]{1,0:T(8,128)}, f32[1,512]{1,0:T(1,128)}, /*i...) custom-call(bf16[2,64,16,128]{3,2,1,0:T(8,128)(2,1)} %get-tuple-element.22.grad_a_h, ...), custom_call_target="tpu_custom_call" | custom-call | tf_op jit(solution)/shard_map/pallas_call | solution.py:548

commit v4 on v3

--- a/solution.py
+++ b/solution.py
@@ -32,7 +32,7 @@
     got_values, got_index, weight_v, weight_pair,
     hid_two_v, dense_t, hid_one_t, scale_one, scale_two, deep_v, low_hot, slot_hot,
     logit_send, logit_got, spread, picked, res_send, res_got,
-    block_hot, total, z_out_v, n_out_v,
+    hot_v, value_two, block_hot, total, z_out_v, n_out_v,
     d_one_v, d_two_v, own_one, own_two,
     part_a, pair_a, sum_a, got_a, final_a, full_a, part_b, pair_b, sum_b, got_b, final_b, full_b,
     small_v, small_rep, small_sum, small_blk,
@@ -228,6 +228,14 @@
             for c, turn in ((0, core), (1, other)):
                 send(logit_send.at[turn, b_to * X + x_to], logit_got.at[me], 2, logit_sem, (b_to, x_to * 2 + c))
 
+    half_table = BD // 2
+
+    @pl.loop(0, NP)
+    def _(p):
+        name = merged(got_index, p)
+        low = jnp.where(name < 0, -1, lax.bitwise_and(name, half_table - 1))
+        hot_v[p] = (lax.broadcasted_iota(jnp.int32, (half_table, 128), 0) == low).astype(F32).astype(BF16)
+
     wait_for(logit_got.at[pl.ds(0, ND - 1)], logit_sem)
     eight = lax.broadcasted_iota(jnp.int32, (NH, 128), 0)
     for p in range(NP):
@@ -328,7 +336,15 @@
         send(small_v, small_rep.at[rep], 6, small_sem.at[0], (blk, lax.rem(rep + k, R)))
     small_rep[rep] = small_v[...]
 
-    def hand_out(own, got, final, full, piece, sem_at):
+    @pl.loop(0, NP)
+    def _(p):
+        upper = jnp.broadcast_to((merged(got_index, p) >= half_table).astype(F32), (128, 128)).T
+        values = got_values[pl.ds(2 * p, 2)].reshape(2 * CAP, W).astype(F32)
+        above = values * upper
+        at = pl.multiple_of(p * 128, 128)
+        value_two[pl.ds(at, 128), :] = jnp.concatenate([values - above, above], axis=1).astype(BF16)
+
+    def hand_out(own, got, final, full, out_h, piece, sem_at):
         own.wait()
         wait_for(got.at[pl.ds(0, NC - 1)], rs_sem.at[piece])
         final[...] = lax.fori_loop(
@@ -336,14 +352,14 @@
         ).astype(BF16)
         for m in range(1, NC):
             b_to, x_to = chip_at(m)
-            send(final, full.at[core, chip], sem_at, ag_sem.at[piece, m // 4], (b_to, x_to * 2 + core))
-        send(final, full.at[core, chip], 8 + 5 * piece, fw_sem.at[piece], (blk, rep_other))
-        copy = pltpu.make_async_copy(final, full.at[core, chip], own_sem.at[3 + piece])
+            send(final, full.at[chip], sem_at, ag_sem.at[piece, m // 4], (b_to, x_to * 2 + core))
+        send(final, out_h.at[core, chip], 8 + 5 * piece, fw_sem.at[piece], (blk, rep_other))
+        copy = pltpu.make_async_copy(final, full.at[chip], own_sem.at[3 + piece])
         copy.start()
         return copy
 
-    own_final_a = hand_out(own_a, got_a, final_a, full_a, 0, 7)
-    own_final_b = hand_out(own_b, got_b, final_b, full_b, 1, 12)
+    own_final_a = hand_out(own_a, got_a, final_a, full_a, grad_a_o, 0, 7)
+    own_final_b = hand_out(own_b, got_b, final_b, full_b, grad_b_o, 1, 12)
 
     wait_for(small_rep.at[pl.ds(0, R - 1)], small_sem.at[0])
     acc = small_rep[0]
@@ -357,20 +373,20 @@
     wait_for(res_got.at[pl.ds(0, ND - 1)], res_sem)
     total[...] = jnp.zeros_like(total)
 
-    @pl.loop(0, B)
+    @pl.loop(0, NP // 8)
     def _(g):
-        for h in range(X):
-            p = g * X + h
-            hit = lax.broadcasted_iota(jnp.int32, (BD, 128), 0) == merged(got_index, p)
-            block_hot[:, h * 128:(h + 1) * 128] = jnp.where(hit, merged(res_got, p), 0.0).astype(BF16)
-        values = got_values[pl.ds(g * R, R)].reshape(R * CAP, W)
-        total[...] += mm(block_hot[...], values)
-
-    grad = total[...]
-    n_old = n_v[...]
-    n_new = n_old + grad * grad
-    n_out_v[...] = n_new
-    z_out_v[...] = z_v[...] + grad - (jnp.sqrt(n_new) - jnp.sqrt(n_old)) / 0.5 * weight_v[...]
+        for h in range(8):
+            p = g * 8 + h
+            block_hot[:, h * 128:(h + 1) * 128] = hot_v[p] * merged(res_got, p).astype(BF16)
+        total[...] += mm(block_hot[...], value_two[pl.ds(pl.multiple_of(g * 1024, 1024), 1024), :])
+
+    for h in range(2):
+        span = slice(h * half_table, (h + 1) * half_table)
+        grad = total[:, h * W:(h + 1) * W]
+        n_old = n_v[span, :]
+        n_new = n_old + grad * grad
+        n_out_v[span, :] = n_new
+        z_out_v[span, :] = z_v[span, :] + grad - (jnp.sqrt(n_new) - jnp.sqrt(n_old)) / 0.5 * weight_v[span, :]
     out_z = pltpu.make_async_copy(z_out_v, z_o, out_sem.at[0])
     out_z.start()
     out_n = pltpu.make_async_copy(n_out_v, n_o, out_sem.at[1])
@@ -382,7 +398,7 @@
         def pass_on(m):
             b_from, x_from = chip_from(m)
             q = b_from * X + x_from
-            send(full.at[core, q], full.at[core, q], 8 + 5 * piece, fw_sem.at[piece], (blk, rep_other))
+            send(full.at[q], out_h.at[core, q], 8 + 5 * piece, fw_sem.at[piece], (blk, rep_other))
 
         wait_for(got.at[pl.ds(0, 3)], ag_sem.at[piece, 0])
         for m in range(1, 4):
@@ -394,7 +410,7 @@
             for i in range(4):
                 pass_on(4 * g + i)
 
-        copy = pltpu.make_async_copy(full.at[core], out_h.at[core], out_sem.at[2 + piece])
+        copy = pltpu.make_async_copy(full, out_h.at[core], out_sem.at[2 + piece])
         copy.start()
         return copy
 
@@ -406,11 +422,7 @@
         acc = acc + small_blk[r]
     small_o[...] = acc
     wait_for(got_a, fw_sem.at[0])
-    out_c = pltpu.make_async_copy(full_a.at[other], grad_a_o.at[other], out_sem.at[4])
-    out_c.start()
     wait_for(got_b, fw_sem.at[1])
-    out_d = pltpu.make_async_copy(full_b.at[other], grad_b_o.at[other], out_sem.at[5])
-    out_d.start()
 
     wait_for(got_index.at[pl.ds(0, ND - 1)], send_sem.at[0])
     wait_for(got_values.at[pl.ds(0, ND - 1)], send_sem.at[1])
@@ -426,7 +438,7 @@
     wait_for(got_b.at[pl.ds(0, NC - 1)], send_sem.at[12])
     wait_for(got_b, send_sem.at[13])
     wait_for(small_blk.at[pl.ds(0, B - 1)], send_sem.at[9])
-    for copy in (out_z, out_n, out_a, out_b, out_c, out_d):
+    for copy in (out_z, out_n, out_a, out_b):
         copy.wait()
 
 
@@ -508,7 +520,7 @@
 
         def slabs(high):
             each = V((NC, high, 128), BF16)
-            return each, each, each, each, V((high, 128), BF16), V((2, NC, high, 128), BF16)
+            return each, each, each, each, V((high, 128), BF16), each
 
         dma = pltpu.SemaphoreType.DMA
         scratch = [
@@ -520,13 +532,13 @@
             V((NH, 128)), V((128, ND * CAP), BF16), V((ND * CAP, 128), BF16),
             V((2, NP, 1, 128)), V((ND, 1, 128)), V((2 * NH, ND * CAP), BF16), V((2 * NH, ND * CAP)),
             V((2, NP, 1, 128)), V((ND, 1, 128)),
-            V((BD, R * CAP), BF16), V((BD, W)), V((BD, W)), V((BD, W)),
+            V((NP, BD // 2, 128), BF16), V((ND * CAP, 2 * W), BF16), V((BD // 2, 1024), BF16), V((BD // 2, 2 * W)), V((BD, W)), V((BD, W)),
             V((E, H1), BF16), V((E, H2), BF16), V((DIN // 4, H1)), V((H1 // 2, H2)),
             *slabs(c1 // 2), *slabs(c1 // 2 + c2),
             V((8, 128)), V((R, 8, 128)), V((8, 128)), V((B, 8, 128)),
             dma((12,)), dma((5,)), pltpu.SemaphoreType.REGULAR, dma((NC // 2,)), dma((NC // 2,)), dma(()), dma(()),
             dma((2,)), dma((2,)), dma((2, NC // 4)), dma((2,)), dma((2,)),
-            dma((14,)), dma((6,)),
+            dma((14,)), dma((4,)),
         ]
         shape = jax.ShapeDtypeStruct
         prob, z_new, n_new, grad_a, grad_b, small = pl.pallas_call(

time: 79.3 us -> 76.9 us (0.970)
  Pallas kernels: 78.5 us -> 76.1 us
    pallas_call x1, Pallas kernels: 74.2 us -> 71.9 us  [per_device(): pl.pallas_call(functools.partial(step_kernel, B, R), out_shape=(shape((NH...]
where the time goes in v4:
time: 76.9 us; the launch traced here: 76.8 us
  Pallas kernels  76.1 us (99%)
    pallas_call x1, Pallas kernels, per_device(): pl.pallas_call(functools.partial(step_kernel, B, R), out_shape=(shape((NH...  71.9 us
    pallas_call x1, Pallas kernels, per_device(): pl.pallas_call(functools.partial(finish_kernel, c1, c2), out_shape=(shape...  4.24 us

profile of v4, /device:TPU:1, one launch (start us, length us, event | category | flops | bytes accessed | tf_op | source)
XLA Modules:
  0.0 76.8 jit_solution(5445371414336262238)
XLA Ops:
  0.6 71.9 %shard_map.188 = (f32[8,128]{1,0:T(8,128)}, f32[1024,128]{1,0:T(8,128)}, f32[1024,128]{1,0:T(8,128)}, bf16[2,64,16,128]{3,2,1,0:T(8,128)(2,1)}, bf16[2,64,24,128]{3,2,1,0:T(8,128)(2,1)}, /*index=5*/f32[8,128]{1,0:T(8,128)}) custom-call(bf16[1024,1024]{1,0:T(8,128)(2,1)} %dense_h.1, s32[8,128]{1,0:T(8,128)} %bitcast.13, bf16[128,64,128]{2,1,0:T(8,128)(2,1)} %values_h.1, ...), custom_call_target="tpu_custom_call" | custom-call | tf_op jit(solution)/shard_map/pallas_call | solution.py:544
  72.5 4.2 %shard_map.189 = (f32[8,128]{1,0:T(8,128)}, f32[1024,128]{1,0:T(8,128)}, f32[1024,128]{1,0:T(8,128)}, f32[1024,512]{1,0:T(8,128)}, f32[1,512]{1,0:T(1,128)}, /*i...) custom-call(bf16[2,64,16,128]{3,2,1,0:T(8,128)(2,1)} %get-tuple-element.22.grad_a_h, ...), custom_call_target="tpu_custom_call" | custom-call | tf_op jit(solution)/shard_map/pallas_call | solution.py:560

commit v5 on v4

--- a/solution.py
+++ b/solution.py
@@ -32,10 +32,10 @@
     got_values, got_index, weight_v, weight_pair,
     hid_two_v, dense_t, hid_one_t, scale_one, scale_two, deep_v, low_hot, slot_hot,
     logit_send, logit_got, spread, picked, res_send, res_got,
-    hot_v, value_two, block_hot, total, z_out_v, n_out_v,
+    names_v, hot_v, value_two, block_hot, total, z_out_v, n_out_v,
     d_one_v, d_two_v, own_one, own_two,
     part_a, pair_a, sum_a, got_a, final_a, full_a, part_b, pair_b, sum_b, got_b, final_b, full_b,
-    small_v, small_rep, small_sum, small_blk,
+    small_v, small_rep, small_sum, small_blk, small_all, prob_v,
     load_sem, own_sem, ready_sem, index_sem, value_sem, logit_sem, res_sem,
     pair_sem, rs_sem, ag_sem, fw_sem, small_sem,
     send_sem, out_sem,
@@ -67,15 +67,22 @@
     z_at = [lax.rem(zz + i, Z) for i in range(Z)]
     x_at = [lax.rem(x + i, X) for i in range(X)]
 
+    def spread_of(spot):
+        return spot // (Z * X), spot // X % Z, spot % X
+
+    def hops(spot):
+        return sum(min(d, n - d) for d, n in zip(spread_of(spot), (Y, Z, X)))
+
+    strided = [(m * STRIDE) % NC for m in range(NC)]
+    order = [q for q in strided if q < X] + sorted([q for q in strided if q >= X], key=lambda q: -hops(q))
+
     def chip_at(m):
-        spot = (m * STRIDE) % NC
-        dy, dz, dx = spot // (Z * X), spot // X % Z, spot % X
+        dy, dz, dx = spread_of(order[m])
         return y_at[dy] + z_at[dz], x_at[dx]
 
     def chip_from(m):
-        spot = lax.rem(m * STRIDE, NC)
-        dy, dz, dx = lax.div(spot, Z * X), lax.rem(lax.div(spot, X), Z), lax.rem(spot, X)
-        return lax.rem(y + Y - dy, Y) * Z + lax.rem(zz + Z - dz, Z), lax.rem(x + X - dx, X)
+        dy, dz, dx = spread_of(order[m])
+        return y_at[(Y - dy) % Y] + z_at[(Z - dz) % Z], x_at[(X - dx) % X]
 
     loads = [
         (block_h, block_v), (count_h, count_v), (example_h, example_t), (z_h, z_v), (n_h, n_v), (dense_h, dense_v),
@@ -125,7 +132,7 @@
 
     give(0, other)
     for m in range(1, NC):
-        spot = (m * STRIDE) % NC
+        spot = order[m]
         if spot < X:
             give(m, 0)
             give(m, 1)
@@ -139,7 +146,7 @@
     pl.semaphore_wait(ready_sem, R - 1)
 
     for m in range(1, NC):
-        spot = (m * STRIDE) % NC
+        spot = order[m]
         if spot >= X and spot % X == 0:
             give(m, other)
         elif spot >= X:
@@ -218,8 +225,7 @@
         send(logit_send.at[turn, b_next * X + x_next], logit_got.at[me], 2, logit_sem, (b_next, x_next * 2 + c))
     logit_got[me] = logit_send[0, chip]
 
-    @pl.loop(1, NC // 2)
-    def _(u):
+    for u in range(1, NC // 2):
         wait_for(got_index.at[pl.ds(0, 4)], index_sem.at[u])
         wait_for(got_values.at[pl.ds(0, 4)], value_sem.at[u])
         places = [chip_from(2 * u), chip_from(2 * u + 1)]
@@ -235,6 +241,15 @@
         name = merged(got_index, p)
         low = jnp.where(name < 0, -1, lax.bitwise_and(name, half_table - 1))
         hot_v[p] = (lax.broadcasted_iota(jnp.int32, (half_table, 128), 0) == low).astype(F32).astype(BF16)
+
+    for p in range(NP):
+        names_v[p:p + 1, :] = (merged(got_index, p) >= half_table).astype(F32)
+    upper = names_v[...].T
+    for p in range(NP):
+        values = got_values[2 * p:2 * p + 2].reshape(2 * CAP, W).astype(F32)
+        above = values * upper[:, p:p + 1]
+        value_two[p * 128:(p + 1) * 128, 0:W] = (values - above).astype(BF16)
+        value_two[p * 128:(p + 1) * 128, W:2 * W] = above.astype(BF16)
 
     wait_for(logit_got.at[pl.ds(0, ND - 1)], logit_sem)
     eight = lax.broadcasted_iota(jnp.int32, (NH, 128), 0)
@@ -245,7 +260,9 @@
         spread[:, p * 128:(p + 1) * 128] = jnp.concatenate([top, term - top], axis=0).astype(BF16)
     wide = mm(spread[...], slot_hot[...])
     prob = jax.nn.sigmoid(wide[:NH] + wide[NH:] + deep_v[...])
-    prob_o[...] = prob
+    prob_v[...] = prob
+    out_prob = pltpu.make_async_copy(prob_v, prob_o, out_sem.at[4])
+    out_prob.start()
     residual = prob - labels_v[...].astype(F32)
     dlogit = residual.astype(BF16).astype(F32)
 
@@ -336,14 +353,6 @@
         send(small_v, small_rep.at[rep], 6, small_sem.at[0], (blk, lax.rem(rep + k, R)))
     small_rep[rep] = small_v[...]
 
-    @pl.loop(0, NP)
-    def _(p):
-        upper = jnp.broadcast_to((merged(got_index, p) >= half_table).astype(F32), (128, 128)).T
-        values = got_values[pl.ds(2 * p, 2)].reshape(2 * CAP, W).astype(F32)
-        above = values * upper
-        at = pl.multiple_of(p * 128, 128)
-        value_two[pl.ds(at, 128), :] = jnp.concatenate([values - above, above], axis=1).astype(BF16)
-
     def hand_out(own, got, final, full, out_h, piece, sem_at):
         own.wait()
         wait_for(got.at[pl.ds(0, NC - 1)], rs_sem.at[piece])
@@ -392,6 +401,14 @@
     out_n = pltpu.make_async_copy(n_out_v, n_o, out_sem.at[1])
     out_n.start()
 
+    wait_for(small_blk.at[pl.ds(0, B - 1)], small_sem.at[1])
+    acc = small_blk[0]
+    for r in range(1, B):
+        acc = acc + small_blk[r]
+    small_all[...] = acc
+    out_small = pltpu.make_async_copy(small_all, small_o, out_sem.at[5])
+    out_small.start()
+
     def pass_all(own, got, full, out_h, piece):
         own.wait()
 
@@ -404,8 +421,7 @@
         for m in range(1, 4):
             pass_on(m)
 
-        @pl.loop(1, NC // 4)
-        def _(g):
+        for g in range(1, NC // 4):
             wait_for(got.at[pl.ds(0, 4)], ag_sem.at[piece, g])
             for i in range(4):
                 pass_on(4 * g + i)
@@ -416,11 +432,6 @@
 
     out_a = pass_all(own_final_a, got_a, full_a, grad_a_o, 0)
     out_b = pass_all(own_final_b, got_b, full_b, grad_b_o, 1)
-    wait_for(small_blk.at[pl.ds(0, B - 1)], small_sem.at[1])
-    acc = small_blk[0]
-    for r in range(1, B):
-        acc = acc + small_blk[r]
-    small_o[...] = acc
     wait_for(got_a, fw_sem.at[0])
     wait_for(got_b, fw_sem.at[1])
 
@@ -438,13 +449,13 @@
     wait_for(got_b.at[pl.ds(0, NC - 1)], send_sem.at[12])
     wait_for(got_b, send_sem.at[13])
     wait_for(small_blk.at[pl.ds(0, B - 1)], send_sem.at[9])
-    for copy in (out_z, out_n, out_a, out_b):
+    for copy in (out_z, out_n, out_a, out_b, out_prob, out_small):
         copy.wait()
 
 
 def finish_kernel(
     c1, c2, grad_a_h, grad_b_h, small_h, prob_h, z_h, n_h, prob_o, z_o, n_o, g_one_o, b_one_o, g_two_o, b_two_o, head_o,
-    grad_a_v, grad_b_v, z_v, n_v, one_v, two_v, in_sem, out_sem,
+    grad_a_v, grad_b_v, z_v, n_v, one_v, two_v, small_v, prob_v, b_one_v, b_two_v, head_v, in_sem, out_sem,
 ):
     NC = grad_a_v.shape[1]
     DIN, H1 = one_v.shape
@@ -458,14 +469,10 @@
         ins.append(pltpu.make_async_copy(grad_b_h.at[h], grad_b_v.at[h], in_sem.at[2 * h + 1]))
     in_z = pltpu.make_async_copy(z_h, z_v, in_sem.at[4])
     in_n = pltpu.make_async_copy(n_h, n_v, in_sem.at[5])
-    for copy in (*ins, in_z, in_n):
+    in_prob = pltpu.make_async_copy(prob_h, prob_v, in_sem.at[6])
+    in_small = pltpu.make_async_copy(small_h, small_v, in_sem.at[7])
+    for copy in (*ins, in_z, in_n, in_prob, in_small):
         copy.start()
-    prob_o[...] = prob_h[...]
-    for q in range(j1):
-        b_one_o[:, q * 128:(q + 1) * 128] = small_h[q:q + 1, :]
-    for q in range(j2):
-        b_two_o[:, q * 128:(q + 1) * 128] = small_h[j1 + q:j1 + q + 1, :]
-        head_o[:, q * 128:(q + 1) * 128] = small_h[j1 + j2 + q:j1 + j2 + q + 1, :]
     outs = []
 
     def out(src, dst):
@@ -490,6 +497,18 @@
             out(z_v, z_o)
             in_n.wait()
             out(n_v, n_o)
+        if h == 0:
+            in_prob.wait()
+            out(prob_v, prob_o)
+            in_small.wait()
+            for q in range(j1):
+                b_one_v[:, q * 128:(q + 1) * 128] = small_v[q:q + 1, :]
+            for q in range(j2):
+                b_two_v[:, q * 128:(q + 1) * 128] = small_v[j1 + q:j1 + q + 1, :]
+                head_v[:, q * 128:(q + 1) * 128] = small_v[j1 + j2 + q:j1 + j2 + q + 1, :]
+            out(b_one_v, b_one_o)
+            out(b_two_v, b_two_o)
+            out(head_v, head_o)
     for copy in outs:
         copy.wait()
 
@@ -512,7 +531,6 @@
         c1 = DIN * H1 // (128 * ND)
         c2 = H1 * H2 // (128 * ND)
         hbm = pl.BlockSpec(memory_space=pl.ANY)
-        vmem = pl.BlockSpec(memory_space=pltpu.VMEM)
         I32 = jnp.int32
 
         def V(shape, kind=F32):
@@ -532,13 +550,13 @@
             V((NH, 128)), V((128, ND * CAP), BF16), V((ND * CAP, 128), BF16),
             V((2, NP, 1, 128)), V((ND, 1, 128)), V((2 * NH, ND * CAP), BF16), V((2 * NH, ND * CAP)),
             V((2, NP, 1, 128)), V((ND, 1, 128)),
-            V((NP, BD // 2, 128), BF16), V((ND * CAP, 2 * W), BF16), V((BD // 2, 1024), BF16), V((BD // 2, 2 * W)), V((BD, W)), V((BD, W)),
+            V((NP, 128)), V((NP, BD // 2, 128), BF16), V((ND * CAP, 2 * W), BF16), V((BD // 2, 1024), BF16), V((BD // 2, 2 * W)), V((BD, W)), V((BD, W)),
             V((E, H1), BF16), V((E, H2), BF16), V((DIN // 4, H1)), V((H1 // 2, H2)),
             *slabs(c1 // 2), *slabs(c1 // 2 + c2),
-            V((8, 128)), V((R, 8, 128)), V((8, 128)), V((B, 8, 128)),
+            V((8, 128)), V((R, 8, 128)), V((8, 128)), V((B, 8, 128)), V((8, 128)), V((NH, 128)),
             dma((12,)), dma((5,)), pltpu.SemaphoreType.REGULAR, dma((NC // 2,)), dma((NC // 2,)), dma(()), dma(()),
             dma((2,)), dma((2,)), dma((2, NC // 4)), dma((2,)), dma((2,)),
-            dma((14,)), dma((4,)),
+            dma((14,)), dma((6,)),
         ]
         shape = jax.ShapeDtypeStruct
         prob, z_new, n_new, grad_a, grad_b, small = pl.pallas_call(
@@ -548,7 +566,7 @@
                 shape((2, NC, c1 // 2, 128), BF16), shape((2, NC, c1 // 2 + c2, 128), BF16), shape((8, 128), F32),
             ),
             in_specs=[hbm] * 13,
-            out_specs=(vmem, hbm, hbm, hbm, hbm, vmem),
+            out_specs=(hbm,) * 6,
             scratch_shapes=scratch,
             compiler_params=pltpu.CompilerParams(
                 collective_id=0, has_side_effects=True, vmem_limit_bytes=60 * 1024 * 1024
@@ -563,11 +581,12 @@
                 shape((NH, 128), F32), shape((BD, W), F32), shape((BD, W), F32), shape((DIN, H1), F32),
                 shape((1, H1), F32), shape((H1, H2), F32), shape((1, H2), F32), shape((1, H2), F32),
             ),
-            in_specs=[hbm, hbm, vmem, vmem, hbm, hbm],
-            out_specs=(vmem, hbm, hbm, hbm, vmem, hbm, vmem, vmem),
+            in_specs=[hbm] * 6,
+            out_specs=(hbm,) * 8,
             scratch_shapes=[
                 V((2, NC, c1 // 2, 128), BF16), V((2, NC, c1 // 2 + c2, 128), BF16), V((BD, W)), V((BD, W)),
-                V((DIN, H1)), V((H1, H2)), dma((6,)), dma((8,)),
+                V((DIN, H1)), V((H1, H2)), V((8, 128)), V((NH, 128)), V((1, H1)), V((1, H2)), V((1, H2)),
+                dma((8,)), dma((12,)),
             ],
             compiler_params=pltpu.CompilerParams(vmem_limit_bytes=63 * 1024 * 1024),
         )(grad_a, grad_b, small, prob, z_new, n_new)

time: 76.9 us -> 77.7 us (1.010)
    pallas_call x1, Pallas kernels: 71.9 us -> 73.7 us  [per_device(): pl.pallas_call(functools.partial(step_kernel, B, R), out_shape=(shape((NH...]
    pallas_call x1, Pallas kernels: 4.24 us -> 3.02 us  [per_device(): pl.pallas_call(functools.partial(finish_kernel, c1, c2), out_shape=(shape...]
where the time goes in v5:
time: 77.7 us; the launch traced here: 77.5 us
  Pallas kernels  76.7 us (99%)
  between operations  0.81 us (1%)
    pallas_call x1, Pallas kernels, per_device(): pl.pallas_call(functools.partial(step_kernel, B, R), out_shape=(shape((NH...  73.7 us
    pallas_call x1, Pallas kernels, per_device(): pl.pallas_call(functools.partial(finish_kernel, c1, c2), out_shape=(shape...  3.02 us

profile of v5, /device:TPU:1, one launch (start us, length us, event | category | flops | bytes accessed | tf_op | source)
XLA Modules:
  0.0 77.5 jit_solution(5442500458178698124)
XLA Ops:
  0.6 73.7 %shard_map.188 = (f32[8,128]{1,0:T(8,128)}, f32[1024,128]{1,0:T(8,128)}, f32[1024,128]{1,0:T(8,128)}, bf16[2,64,16,128]{3,2,1,0:T(8,128)(2,1)}, bf16[2,64,24,128]{3,2,1,0:T(8,128)(2,1)}, /*index=5*/f32[8,128]{1,0:T(8,128)}) custom-call(bf16[1024,1024]{1,0:T(8,128)(2,1)} %dense_h.1, s32[8,128]{1,0:T(8,128)} %bitcast.13, bf16[128,64,128]{2,1,0:T(8,128)(2,1)} %values_h.1, ...), custom_call_target="tpu_custom_call" | custom-call | tf_op jit(solution)/shard_map/pallas_call | solution.py:562
  74.3 3.0 %shard_map.189 = (f32[8,128]{1,0:T(8,128)}, f32[1024,128]{1,0:T(8,128)}, f32[1024,128]{1,0:T(8,128)}, f32[1024,512]{1,0:T(8,128)}, f32[1,512]{1,0:T(1,128)}, /*i...) custom-call(bf16[2,64,16,128]{3,2,1,0:T(8,128)(2,1)} %get-tuple-element.22.grad_a_h, ...), custom_call_target="tpu_custom_call" | custom-call | tf_op jit(solution)/shard_map/pallas_call | solution.py:578

commit v6 on v5

--- a/solution.py
+++ b/solution.py
@@ -32,7 +32,7 @@
     got_values, got_index, weight_v, weight_pair,
     hid_two_v, dense_t, hid_one_t, scale_one, scale_two, deep_v, low_hot, slot_hot,
     logit_send, logit_got, spread, picked, res_send, res_got,
-    names_v, hot_v, value_two, block_hot, total, z_out_v, n_out_v,
+    names_v, value_two, block_hot, total, z_out_v, n_out_v,
     d_one_v, d_two_v, own_one, own_two,
     part_a, pair_a, sum_a, got_a, final_a, full_a, part_b, pair_b, sum_b, got_b, final_b, full_b,
     small_v, small_rep, small_sum, small_blk, small_all, prob_v,
@@ -67,14 +67,10 @@
     z_at = [lax.rem(zz + i, Z) for i in range(Z)]
     x_at = [lax.rem(x + i, X) for i in range(X)]
 
+    order = [(m * STRIDE) % NC for m in range(NC)]
+
     def spread_of(spot):
         return spot // (Z * X), spot // X % Z, spot % X
-
-    def hops(spot):
-        return sum(min(d, n - d) for d, n in zip(spread_of(spot), (Y, Z, X)))
-
-    strided = [(m * STRIDE) % NC for m in range(NC)]
-    order = [q for q in strided if q < X] + sorted([q for q in strided if q >= X], key=lambda q: -hops(q))
 
     def chip_at(m):
         dy, dz, dx = spread_of(order[m])
@@ -236,21 +232,6 @@
 
     half_table = BD // 2
 
-    @pl.loop(0, NP)
-    def _(p):
-        name = merged(got_index, p)
-        low = jnp.where(name < 0, -1, lax.bitwise_and(name, half_table - 1))
-        hot_v[p] = (lax.broadcasted_iota(jnp.int32, (half_table, 128), 0) == low).astype(F32).astype(BF16)
-
-    for p in range(NP):
-        names_v[p:p + 1, :] = (merged(got_index, p) >= half_table).astype(F32)
-    upper = names_v[...].T
-    for p in range(NP):
-        values = got_values[2 * p:2 * p + 2].reshape(2 * CAP, W).astype(F32)
-        above = values * upper[:, p:p + 1]
-        value_two[p * 128:(p + 1) * 128, 0:W] = (values - above).astype(BF16)
-        value_two[p * 128:(p + 1) * 128, W:2 * W] = above.astype(BF16)
-
     wait_for(logit_got.at[pl.ds(0, ND - 1)], logit_sem)
     eight = lax.broadcasted_iota(jnp.int32, (NH, 128), 0)
     for p in range(NP):
@@ -379,6 +360,15 @@
         send(small_sum, small_blk.at[blk], 9, small_sem.at[1], (lax.rem(blk + k, B), rep))
     small_blk[blk] = acc
 
+    for p in range(NP):
+        names_v[p:p + 1, :] = (merged(got_index, p) >= half_table).astype(F32)
+    upper = names_v[...].T
+    for p in range(NP):
+        values = got_values[2 * p:2 * p + 2].reshape(2 * CAP, W)
+        above = values * jnp.broadcast_to(upper[:, p:p + 1], (2 * CAP, W)).astype(BF16)
+        value_two[p * 128:(p + 1) * 128, 0:W] = values - above
+        value_two[p * 128:(p + 1) * 128, W:2 * W] = above
+
     wait_for(res_got.at[pl.ds(0, ND - 1)], res_sem)
     total[...] = jnp.zeros_like(total)
 
@@ -386,7 +376,10 @@
     def _(g):
         for h in range(8):
             p = g * 8 + h
-            block_hot[:, h * 128:(h + 1) * 128] = hot_v[p] * merged(res_got, p).astype(BF16)
+            name = merged(got_index, p)
+            low = jnp.where(name < 0, -1, lax.bitwise_and(name, half_table - 1))
+            hit = lax.broadcasted_iota(jnp.int32, (half_table, 128), 0) == low
+            block_hot[:, h * 128:(h + 1) * 128] = jnp.where(hit, merged(res_got, p), 0.0).astype(BF16)
         total[...] += mm(block_hot[...], value_two[pl.ds(pl.multiple_of(g * 1024, 1024), 1024), :])
 
     for h in range(2):
@@ -550,7 +543,7 @@
             V((NH, 128)), V((128, ND * CAP), BF16), V((ND * CAP, 128), BF16),
             V((2, NP, 1, 128)), V((ND, 1, 128)), V((2 * NH, ND * CAP), BF16), V((2 * NH, ND * CAP)),
             V((2, NP, 1, 128)), V((ND, 1, 128)),
-            V((NP, 128)), V((NP, BD // 2, 128), BF16), V((ND * CAP, 2 * W), BF16), V((BD // 2, 1024), BF16), V((BD // 2, 2 * W)), V((BD, W)), V((BD, W)),
+            V((NP, 128)), V((ND * CAP, 2 * W), BF16), V((BD // 2, 1024), BF16), V((BD // 2, 2 * W)), V((BD, W)), V((BD, W)),
             V((E, H1), BF16), V((E, H2), BF16), V((DIN // 4, H1)), V((H1 // 2, H2)),
             *slabs(c1 // 2), *slabs(c1 // 2 + c2),
             V((8, 128)), V((R, 8, 128)), V((8, 128)), V((B, 8, 128)), V((8, 128)), V((NH, 128)),

time: 77.7 us -> 75.5 us (0.972)
  Pallas kernels: 76.7 us -> 74.6 us
    pallas_call x1, Pallas kernels: 73.7 us -> 71.5 us  [per_device(): pl.pallas_call(functools.partial(step_kernel, B, R), out_shape=(shape((NH...]
where the time goes in v6:
time: 75.5 us; the launch traced here: 75.4 us
  Pallas kernels  74.6 us (99%)
  between operations  0.83 us (1%)
    pallas_call x1, Pallas kernels, per_device(): pl.pallas_call(functools.partial(step_kernel, B, R), out_shape=(shape((NH...  71.5 us
    pallas_call x1, Pallas kernels, per_device(): pl.pallas_call(functools.partial(finish_kernel, c1, c2), out_shape=(shape...  3.02 us

profile of v6, /device:TPU:1, one launch (start us, length us, event | category | flops | bytes accessed | tf_op | source)
XLA Modules:
  0.0 75.4 jit_solution(2426777513220664217)
XLA Ops:
  0.6 71.5 %shard_map.188 = (f32[8,128]{1,0:T(8,128)}, f32[1024,128]{1,0:T(8,128)}, f32[1024,128]{1,0:T(8,128)}, bf16[2,64,16,128]{3,2,1,0:T(8,128)(2,1)}, bf16[2,64,24,128]{3,2,1,0:T(8,128)(2,1)}, /*index=5*/f32[8,128]{1,0:T(8,128)}) custom-call(bf16[1024,1024]{1,0:T(8,128)(2,1)} %dense_h.1, s32[8,128]{1,0:T(8,128)} %bitcast.13, bf16[128,64,128]{2,1,0:T(8,128)(2,1)} %values_h.1, ...), custom_call_target="tpu_custom_call" | custom-call | tf_op jit(solution)/shard_map/pallas_call | solution.py:555
  72.2 3.0 %shard_map.189 = (f32[8,128]{1,0:T(8,128)}, f32[1024,128]{1,0:T(8,128)}, f32[1024,128]{1,0:T(8,128)}, f32[1024,512]{1,0:T(8,128)}, f32[1,512]{1,0:T(1,128)}, /*i...) custom-call(bf16[2,64,16,128]{3,2,1,0:T(8,128)(2,1)} %get-tuple-element.22.grad_a_h, ...), custom_call_target="tpu_custom_call" | custom-call | tf_op jit(solution)/shard_map/pallas_call | solution.py:571

commit v7 on v6

--- a/solution.py
+++ b/solution.py
@@ -77,8 +77,9 @@
         return y_at[dy] + z_at[dz], x_at[dx]
 
     def chip_from(m):
-        dy, dz, dx = spread_of(order[m])
-        return y_at[(Y - dy) % Y] + z_at[(Z - dz) % Z], x_at[(X - dx) % X]
+        spot = lax.rem(m * STRIDE, NC)
+        dy, dz, dx = lax.div(spot, Z * X), lax.rem(lax.div(spot, X), Z), lax.rem(spot, X)
+        return lax.rem(y + Y - dy, Y) * Z + lax.rem(zz + Z - dz, Z), lax.rem(x + X - dx, X)
 
     loads = [
         (block_h, block_v), (count_h, count_v), (example_h, example_t), (z_h, z_v), (n_h, n_v), (dense_h, dense_v),
@@ -221,7 +222,8 @@
         send(logit_send.at[turn, b_next * X + x_next], logit_got.at[me], 2, logit_sem, (b_next, x_next * 2 + c))
     logit_got[me] = logit_send[0, chip]
 
-    for u in range(1, NC // 2):
+    @pl.loop(1, NC // 2)
+    def _(u):
         wait_for(got_index.at[pl.ds(0, 4)], index_sem.at[u])
         wait_for(got_values.at[pl.ds(0, 4)], value_sem.at[u])
         places = [chip_from(2 * u), chip_from(2 * u + 1)]
@@ -414,7 +416,8 @@
         for m in range(1, 4):
             pass_on(m)
 
-        for g in range(1, NC // 4):
+        @pl.loop(1, NC // 4)
+        def _(g):
             wait_for(got.at[pl.ds(0, 4)], ag_sem.at[piece, g])
             for i in range(4):
                 pass_on(4 * g + i)

time: 75.5 us -> 75.1 us (level)
  no operation moved by 1% of the time
where the time goes in v7:
time: 75.1 us; the launch traced here: 74.9 us
  Pallas kernels  74.3 us (99%)
    pallas_call x1, Pallas kernels, per_device(): pl.pallas_call(functools.partial(step_kernel, B, R), out_shape=(shape((NH...  71.2 us
    pallas_call x1, Pallas kernels, per_device(): pl.pallas_call(functools.partial(finish_kernel, c1, c2), out_shape=(shape...  3.02 us

profile of v7, /device:TPU:1, one launch (start us, length us, event | category | flops | bytes accessed | tf_op | source)
XLA Modules:
  0.0 74.9 jit_solution(14430752769478876448)
XLA Ops:
  0.6 71.2 %shard_map.188 = (f32[8,128]{1,0:T(8,128)}, f32[1024,128]{1,0:T(8,128)}, f32[1024,128]{1,0:T(8,128)}, bf16[2,64,16,128]{3,2,1,0:T(8,128)(2,1)}, bf16[2,64,24,128]{3,2,1,0:T(8,128)(2,1)}, /*index=5*/f32[8,128]{1,0:T(8,128)}) custom-call(bf16[1024,1024]{1,0:T(8,128)(2,1)} %dense_h.1, s32[8,128]{1,0:T(8,128)} %bitcast.13, bf16[128,64,128]{2,1,0:T(8,128)(2,1)} %values_h.1, ...), custom_call_target="tpu_custom_call" | custom-call | tf_op jit(solution)/shard_map/pallas_call | solution.py:558
  71.9 3.0 %shard_map.189 = (f32[8,128]{1,0:T(8,128)}, f32[1024,128]{1,0:T(8,128)}, f32[1024,128]{1,0:T(8,128)}, f32[1024,512]{1,0:T(8,128)}, f32[1,512]{1,0:T(1,128)}, /*i...) custom-call(bf16[2,64,16,128]{3,2,1,0:T(8,128)(2,1)} %get-tuple-element.22.grad_a_h, ...), custom_call_target="tpu_custom_call" | custom-call | tf_op jit(solution)/shard_map/pallas_call | solution.py:574

commit v8 on v7

--- a/solution.py
+++ b/solution.py
@@ -11,7 +11,7 @@
 F32 = jnp.float32
 BF16 = jnp.bfloat16
 NT = (((1,), (1,)), ((), ()))
-STRIDE = 27
+STRIDE = 37
 
 
 def mm(a, b):

time: 75.1 us -> 75.2 us (level)
  no operation moved by 1% of the time
where the time goes in v8:
time: 75.2 us; the launch traced here: 75.1 us
  Pallas kernels  74.5 us (99%)
    pallas_call x1, Pallas kernels, per_device(): pl.pallas_call(functools.partial(step_kernel, B, R), out_shape=(shape((NH...  71.4 us
    pallas_call x1, Pallas kernels, per_device(): pl.pallas_call(functools.partial(finish_kernel, c1, c2), out_shape=(shape...  3.02 us

profile of v8, /device:TPU:1, one launch (start us, length us, event | category | flops | bytes accessed | tf_op | source)
XLA Modules:
  0.0 75.1 jit_solution(2333034989269369407)
XLA Ops:
  0.6 71.4 %shard_map.188 = (f32[8,128]{1,0:T(8,128)}, f32[1024,128]{1,0:T(8,128)}, f32[1024,128]{1,0:T(8,128)}, bf16[2,64,16,128]{3,2,1,0:T(8,128)(2,1)}, bf16[2,64,24,128]{3,2,1,0:T(8,128)(2,1)}, /*index=5*/f32[8,128]{1,0:T(8,128)}) custom-call(bf16[1024,1024]{1,0:T(8,128)(2,1)} %dense_h.1, s32[8,128]{1,0:T(8,128)} %bitcast.13, bf16[128,64,128]{2,1,0:T(8,128)(2,1)} %values_h.1, ...), custom_call_target="tpu_custom_call" | custom-call | tf_op jit(solution)/shard_map/pallas_call | solution.py:558
  72.1 3.0 %shard_map.189 = (f32[8,128]{1,0:T(8,128)}, f32[1024,128]{1,0:T(8,128)}, f32[1024,128]{1,0:T(8,128)}, f32[1024,512]{1,0:T(8,128)}, f32[1,512]{1,0:T(1,128)}, /*i...) custom-call(bf16[2,64,16,128]{3,2,1,0:T(8,128)(2,1)} %get-tuple-element.22.grad_a_h, ...), custom_call_target="tpu_custom_call" | custom-call | tf_op jit(solution)/shard_map/pallas_call | solution.py:574
